TPU v7x, 32 devices: a whole 2x2x4 slice. The times are simulated.
32 devices in a mesh: row: 4 (over y, core), col: 8 (over z, x).
Axes of the slice: x: 2, y: 2, z: 4, core: 2. Of those that a mesh axis runs over, the one named last changes fastest.
Arguments:
- coeffs: float32 [2048, 2048], P('row', 'col'), may hold values from -8 to 8, as said below
- features: float32 [2048, 512], P('row'), may hold values from -0.6 to 0.6
- factors: float32 [2048, 256], P('row'), may hold values from -1.8 to 1.8
Outputs:
- grad_coeffs: float32 [2048, 2048], P('row', 'col')
- grad_features: float32 [2048, 512], P('row', 'col')
Inputs may be any that keep to these rules, and one draw needn't show every extreme that they name: `coeffs`: real coefficients.
All inputs are finite; a program needn't handle non-finite values.
Results may differ from a plain program's by a relative error of at most 0.0003.
Values sent between devices are 32-bit elements; how exact they have to be, the bound alone decides.
No kernel may reach another device: no remote copies, remote signals or barrier semaphores. Data moves between devices by JAX's collectives and lax.ppermute only.
A program may use at most 64 MiB of HBM per device.

v0:
```python
import functools
import jax
import jax.numpy as jnp
from jax import lax
from jax.experimental import pallas as pl
from jax.experimental.pallas import tpu as pltpu
from jax.sharding import PartitionSpec as P


AXES = ("row", "col")
F32, BF16 = jnp.float32, jnp.bfloat16


def after(value, *others):
    return lax.optimization_barrier((value, *others))[0]


def split(value):
    high = value.astype(BF16)
    return high, (value - high.astype(F32)).astype(BF16)


def dot3(left, right, left_dim, right_dim):
    def one(a, b):
        return lax.dot_general(
            a, b, (((left_dim,), (right_dim,)), ((), ())), preferred_element_type=F32
        )

    return one(left[0], right[0]) + (one(left[0], right[1]) + one(left[1], right[0]))


def place(fold):
    col = lax.axis_index("col")
    return lax.axis_index("row"), lax.div(col, fold), lax.rem(col, fold)


def identity(first, shape):
    rows = lax.broadcasted_iota(jnp.int32, shape, 0)
    cols = lax.broadcasted_iota(jnp.int32, shape, 1)
    return jnp.where(rows - cols == first, 1.0, 0.0)


def rows_at(start, count):
    return pl.ds(pl.multiple_of(start, count), count)


def call(kernel, outs, args, scratch=(), flops=0, hbm=(), grant=2):
    moved = sum(4 * a.size for a in args) + sum(4 * o.size for o in outs)
    spaces = [pltpu.HBM if n in hbm else pltpu.VMEM for n in range(len(args))]
    return pl.pallas_call(
        kernel,
        out_shape=outs,
        in_specs=[pl.BlockSpec(memory_space=space) for space in spaces],
        out_specs=[pl.BlockSpec(memory_space=pltpu.VMEM) for _ in outs],
        scratch_shapes=list(scratch),
        compiler_params=pltpu.CompilerParams(vmem_limit_bytes=grant << 20),
        cost_estimate=pl.CostEstimate(flops=flops, bytes_accessed=moved, transcendentals=0),
    )(*args)


def shape(*dims, dtype=F32):
    return jax.ShapeDtypeStruct(dims, dtype)


def cut_kernel(cuts, fold, *refs):
    count = max(cut[0] for cut in cuts) + 1
    ins, outs, sems = refs[:count], refs[count:-1], refs[-1]
    r, q, b = place(fold)
    copies = []
    for n, (source, rows, block) in enumerate(cuts):
        copies.append(
            pltpu.make_async_copy(
                ins[source].at[rows_at(block(r, q, b) * rows, rows)], outs[n], sems.at[n]
            )
        )
    for copy in copies:
        copy.start()
    for copy in copies:
        copy.wait()


def cut_rows(arrays, cuts, fold):
    outs = [shape(rows, arrays[source].shape[1]) for source, rows, _ in cuts]
    return call(
        functools.partial(cut_kernel, cuts, fold),
        outs,
        arrays,
        scratch=[pltpu.SemaphoreType.DMA((len(cuts),))],
        hbm=range(len(arrays)),
    )


def residual_kernel(count, fold, *refs):
    parts, blocks, outs, total = refs[:count], refs[count : 2 * count], refs[2 * count : -1], refs[-1]
    r, q, b = place(fold)
    quarter, own_cols = parts[0].shape
    piece = quarter // fold
    for t in range(count):
        wanted = q ^ r ^ t
        left = parts[0][...]
        for s in range(1, count):
            left = jnp.where(wanted == s, parts[s][...], left)
        if t == 0:
            left = left - identity(b * own_cols - q * quarter, left.shape)
        product = dot3(split(left), split(blocks[t][...]), 1, 0)
        if t == 0:
            total[...] = product
        else:
            total[...] += product
    for d in range(fold):
        outs[d][...] = total[rows_at((b ^ d) * piece, piece)]


def assemble(chunks, high, low, fold, q, b):
    piece = chunks[0].shape[0]
    for n, chunk in enumerate(chunks):
        at = rows_at(((q ^ (n // fold)) * fold + (b ^ (n % fold))) * piece, piece)
        high[at], low[at] = split(chunk[...])


def add_kernel(left, right, out):
    out[...] = left[...] + right[...]


def pick_kernel(bit, fold, old_ref, got_ref, out):
    r, q, _ = place(fold)
    out[...] = jnp.where(((r ^ q) & (2 * bit - 1)) == bit, got_ref[...], old_ref[...])


def project_kernel(count, fold, *refs):
    chunks, coeffs = refs[: count * fold], refs[count * fold]
    give, keep, total, high, low = refs[count * fold + 1 :]
    r, q, b = place(fold)
    assemble(chunks, high, low, fold, q, b)
    own_rows, own_cols = coeffs.shape
    less_one = coeffs[...] - identity((q * fold + b) * own_cols - r * own_rows, coeffs.shape)
    total[...] = dot3((high[...], low[...]), split(less_one), 0, 0)
    half = give.shape[0]
    mine = r & 1
    give[...] = total[rows_at((1 - mine) * half, half)]
    keep[...] = total[rows_at(mine * half, half)]


def halve_kernel(bit, fold, old_ref, got_ref, give, keep, total):
    r, _, _ = place(fold)
    total[...] = old_ref[...] + got_ref[...]
    half = give.shape[0]
    mine = lax.rem(lax.div(r, bit), 2)
    give[...] = total[rows_at((1 - mine) * half, half)]
    keep[...] = total[rows_at(mine * half, half)]


def share_kernel(fold, old_ref, got_ref, *refs):
    outs, total = refs[:-1], refs[-1]
    _, _, b = place(fold)
    total[...] = old_ref[...] + got_ref[...]
    width = outs[0].shape[0]
    for d in range(fold):
        outs[d][...] = total[rows_at((b ^ d) * width, width)]


def finish_kernel(fold, *refs):
    parts, out = refs[:fold], refs[fold]
    _, _, b = place(fold)
    cols = parts[0].shape[1]
    for e in range(fold):
        value = parts[0][...]
        for d in range(1, fold):
            value = jnp.where((b ^ e) == d, parts[d][...], value)
        out[:, e * cols : (e + 1) * cols] = value


def coeff_kernel(count, fold, *refs):
    coeffs, factors, col_factors = refs[:3]
    blocks, mirrored = refs[3 : 3 + count], refs[3 + count : 3 + count + fold]
    chunks, (out, high, low) = refs[3 + count + fold : -3], refs[-3:]
    r, q, b = place(fold)
    assemble(chunks, high, low, fold, q, b)
    features = blocks[0][...]
    for t in range(1, count):
        features = jnp.where((r ^ q) == t, blocks[t][...], features)
    features = split(features)
    right = split(col_factors[...])
    rows = mirrored[0].shape[0]
    for e in range(fold):
        at = slice(e * rows, (e + 1) * rows)
        turned = mirrored[0][...]
        for d in range(1, fold):
            turned = jnp.where((b ^ e) == d, mirrored[d][...], turned)
        turned = turned.T
        own = coeffs[at]
        symmetric = 0.5 * (own * own + turned * turned)
        relation = symmetric - dot3(split(factors[at]), right, 1, 1)
        outer = dot3((high[at], low[at]), features, 1, 1)
        out[at] = outer + 2.0 * own * relation


def per_device(coeffs, features, factors):
    row_count = lax.axis_size("row")
    col_count = lax.axis_size("col")
    fold = col_count // row_count
    own_rows, own_cols = coeffs.shape
    width = features.shape[1]
    quarter = own_rows // row_count
    piece = quarter // fold
    bits = [1 << n for n in range(row_count.bit_length() - 1)]
    every, both = range(row_count), range(fold)

    def send(value, route):
        pairs = []
        for i in every:
            for j in every:
                for k in both:
                    to = route(i, j, k)
                    if to is not None:
                        start = i * col_count + j * fold + k
                        pairs.append((start, to[0] * col_count + to[1] * fold + to[2]))
        return lax.ppermute(value, AXES, pairs)

    b = lax.axis_index("col") % fold
    blocks = {0: lax.dynamic_slice_in_dim(features, b * own_cols, own_cols, 0)}
    for bit in reversed(bits):
        for t in list(blocks):
            blocks[t | bit] = send(blocks[t], lambda i, j, k: (i ^ bit, j, k))
    blocks = [blocks[t] for t in every]

    cuts = [(0, quarter, lambda r, q, b, s=s: q ^ s) for s in every]
    cuts += [(0, own_cols, lambda r, q, b, d=d: b ^ d) for d in both]
    cuts += [(1, own_cols, lambda r, q, b: b)]
    cut = cut_rows([coeffs, factors], cuts, fold)
    parts, turns, col_factors = cut[:row_count], cut[row_count:-1], cut[-1]
    parts = [send(parts[s], lambda i, j, k: (i, j ^ s, k)) if s else parts[s] for s in every]

    def mirror(d, *deps):
        return send(after(turns[d], *deps), lambda i, j, k: (j, i, k ^ d))

    mirrored = {fold - 1: mirror(fold - 1, *parts)}

    shares = call(
        functools.partial(residual_kernel, row_count, fold),
        [shape(piece, width)] * fold,
        [*parts, *blocks],
        scratch=[pltpu.VMEM((quarter, width), F32)],
        flops=6 * quarter * row_count * own_cols * width,
        grant=12,
    )
    share = shares[0]
    for d in range(1, fold):
        got = send(shares[d], lambda i, j, k: (i, j, k ^ d))
        share = call(add_kernel, [shape(piece, width)], [share, got])[0]

    col_factors = after(col_factors, blocks[bits[-1]])
    for bit in reversed(bits):
        got = send(
            col_factors, lambda i, j, k: (i ^ bit, j, k) if (i ^ j) & (2 * bit - 1) == 0 else None
        )
        picked = functools.partial(pick_kernel, bit, fold)
        col_factors = call(picked, [shape(*got.shape)], [col_factors, got])[0]

    chunks = [send(share, lambda i, j, k: (i, j ^ s, k)) if s else share for s in every]
    spread = []
    for s in every:
        for d in both:
            one = chunks[s]
            spread.append(send(one, lambda i, j, k: (i, j, k ^ d)) if d else one)
    for d in range(fold - 1):
        mirrored[d] = mirror(d, *chunks)

    halves = [pltpu.VMEM((own_rows, width), BF16)] * 2
    give, keep = call(
        functools.partial(project_kernel, row_count, fold),
        [shape(width // 2, own_cols)] * 2,
        [*spread, coeffs],
        scratch=[pltpu.VMEM((width, own_cols), F32), *halves],
        flops=6 * own_rows * own_cols * width,
        grant=12,
    )
    for bit in bits:
        got = send(give, lambda i, j, k: (i ^ bit, j, k))
        rows = got.shape[0]
        total = pltpu.VMEM((rows, own_cols), F32)
        if bit != bits[-1]:
            give, keep = call(
                functools.partial(halve_kernel, 2 * bit, fold),
                [shape(rows // 2, own_cols)] * 2,
                [keep, got],
                scratch=[total],
            )
    pieces = call(
        functools.partial(share_kernel, fold),
        [shape(rows // fold, own_cols)] * fold,
        [keep, got],
        scratch=[total],
    )

    def turned(i):
        out = 0
        for bit in bits:
            out = 2 * out + (i // bit) % 2
        return out

    placed = [send(pieces[d], lambda i, j, k: (j, turned(i), k ^ d)) for d in both]
    grad_features = call(
        functools.partial(finish_kernel, fold), [shape(rows // fold, own_rows)], placed
    )[0].T

    grad_coeffs = call(
        functools.partial(coeff_kernel, row_count, fold),
        [shape(own_rows, own_cols)],
        [coeffs, factors, col_factors, *blocks, *[mirrored[d] for d in both], *spread],
        scratch=halves,
        flops=6 * own_rows * own_cols * (width + factors.shape[1]),
        grant=12,
    )[0]
    return (grad_coeffs, grad_features)


def solution(mesh):
    in_specs = (P("row", "col"), P("row", None), P("row", None))
    out_specs = (P("row", "col"), P("row", "col"))
    return jax.shard_map(
        per_device, mesh=mesh, in_specs=in_specs, out_specs=out_specs, check_vma=False
    )
```

profile of v0, /device:TPU:4, one launch (start us, length us, event | category | flops | bytes accessed | tf_op | source)
XLA Modules:
  0.0 90.2 jit_solution(13363694048450665957)
XLA Ops:
  0.7 1.2 %copy-done = f32[512,512]{1,0:T(8,128)S(1)} copy-done((f32[512,512]{1,0:T(8,128)S(1)}, f32[512,512]{1,0:T(8,128)}, u32[]{:S(2)}) %copy-start) | copy-done | bytes 1048600
  2.1 13.6 %collective-permute-done.refs_6_.refs_5_ = f32[256,512]{1,0:T(8,128)S(1)} collective-permute-done((f32[256,512]{1,0:T(8,128)S(1)}, f32[256,512]{1,0:T(8,128)S(1)}, u32[]{:S(2)}, u32[]{:S(2)}) %collective-permute-start) | collective-permute-done | bytes 524320 | tf_op jit(solution)/shard_map/ppermute | solution.py:218
  15.6 0.8 shard_map.50
  16.5 1.6 %collective-permute-start.5 = (f32[128,256]{1,0:T(8,128)S(1)}, f32[128,256]{1,0:T(8,128)S(1)}, u32[]{:S(2)}, u32[]{:S(2)}) collective-permute-start(f32[128,256]{1,0:T(8,128)S(1)} %get-tuple-element.24), channel_id=1, source_target_pairs={{0,2},{1,3},{2,0},{3,1},{4,6},{5,7},{6,4},{7,5},{8,10},{9,11},{10,... | collective-permute-start | bytes 393224 | tf_op jit(solution)/shard_map/ppermute | solution.py:218
  18.1 2.6 %collective-permute-start.6 = (f32[128,256]{1,0:T(8,128)S(1)}, f32[128,256]{1,0:T(8,128)S(1)}, u32[]{:S(2)}, u32[]{:S(2)}) collective-permute-start(f32[128,256]{1,0:T(8,128)S(1)} %get-tuple-element.25), channel_id=1, source_target_pairs={{0,4},{1,5},{2,6},{3,7},{4,0},{5,1},{6,2},{7,3},{8,12},{9,13},{10,... | collective-permute-start | bytes 393224 | tf_op jit(solution)/shard_map/ppermute | solution.py:218
  20.9 3.7 %collective-permute-done.5.refs_1_ = f32[128,256]{1,0:T(8,128)S(1)} collective-permute-done((f32[128,256]{1,0:T(8,128)S(1)}, f32[128,256]{1,0:T(8,128)S(1)}, u32[]{:S(2)}, u32[]{:S(2)}) %collective-permute-start.5) | collective-permute-done | bytes 131104 | tf_op jit(solution)/shard_map/ppermute | solution.py:218
  24.7 6.4 %collective-permute-done.6.refs_2_ = f32[128,256]{1,0:T(8,128)S(1)} collective-permute-done((f32[128,256]{1,0:T(8,128)S(1)}, f32[128,256]{1,0:T(8,128)S(1)}, u32[]{:S(2)}, u32[]{:S(2)}) %collective-permute-start.6) | collective-permute-done | bytes 131104 | tf_op jit(solution)/shard_map/ppermute | solution.py:218
  31.1 0.7 shard_map.53
  31.8 1.6 %collective-permute-start.8 = (f32[64,512]{1,0:T(8,128)S(1)}, f32[64,512]{1,0:T(8,128)S(1)}, u32[]{:S(2)}, u32[]{:S(2)}) collective-permute-start(f32[64,512]{1,0:T(8,128)S(1)} %get-tuple-element.28), channel_id=1, source_target_pairs={{0,1},{1,0},{2,3},{3,2},{4,5},{5,4},{6,7},{7,6},{8,9},{9,8},{10,11... | collective-permute-start | bytes 393224 | tf_op jit(solution)/shard_map/ppermute | solution.py:218
  33.4 3.5 %collective-permute-done.8.right = f32[64,512]{1,0:T(8,128)S(1)} collective-permute-done((f32[64,512]{1,0:T(8,128)S(1)}, f32[64,512]{1,0:T(8,128)S(1)}, u32[]{:S(2)}, u32[]{:S(2)}) %collective-permute-start.8) | collective-permute-done | bytes 131104 | tf_op jit(solution)/shard_map/ppermute | solution.py:218
  36.9 2.5 %collective-permute-start.11 = (f32[64,512]{1,0:T(8,128)S(1)}, f32[64,512]{1,0:T(8,128)S(1)}, u32[]{:S(2)}, u32[]{:S(2)}) collective-permute-start(f32[64,512]{1,0:T(8,128)S(1)} %shard_map.54.refs_9_.refs_0_), channel_id=1, source_target_pairs={{0,6},{1,7},{2,4},{3,5},{4,2},{5,3},{6,0},{7,1},{8,14},{9,15},{10,... | collective-permute-start | bytes 393224 | tf_op jit(solution)/shard_map/ppermute | solution.py:218
  39.4 1.6 %collective-permute-start.10 = (f32[64,512]{1,0:T(8,128)S(1)}, f32[64,512]{1,0:T(8,128)S(1)}, u32[]{:S(2)}, u32[]{:S(2)}) collective-permute-start(f32[64,512]{1,0:T(8,128)S(1)} %shard_map.54.refs_9_.refs_0_), channel_id=1, source_target_pairs={{0,4},{1,5},{2,6},{3,7},{4,0},{5,1},{6,2},{7,3},{8,12},{9,13},{10,... | collective-permute-start | bytes 393224 | tf_op jit(solution)/shard_map/ppermute | solution.py:218
  41.3 1.5 %collective-permute-start.14 = (f32[64,512]{1,0:T(8,128)S(1)}, f32[64,512]{1,0:T(8,128)S(1)}, u32[]{:S(2)}, u32[]{:S(2)}) collective-permute-start(f32[64,512]{1,0:T(8,128)S(1)} %shard_map.54.refs_9_.refs_0_), channel_id=1, source_target_pairs={{0,1},{1,0},{2,3},{3,2},{4,5},{5,4},{6,7},{7,6},{8,9},{9,8},{10,11... | collective-permute-start | bytes 393224 | tf_op jit(solution)/shard_map/ppermute | solution.py:218
  42.8 2.3 %collective-permute-done.11.refs_15_.refs_6_ = f32[64,512]{1,0:T(8,128)S(1)} collective-permute-done((f32[64,512]{1,0:T(8,128)S(1)}, f32[64,512]{1,0:T(8,128)S(1)}, u32[]{:S(2)}, u32[]{:S(2)}) %collective-permute-start.11) | collective-permute-done | bytes 131104 | tf_op jit(solution)/shard_map/ppermute | solution.py:218
  45.1 1.5 %collective-permute-start.17 = (f32[64,512]{1,0:T(8,128)S(1)}, f32[64,512]{1,0:T(8,128)S(1)}, u32[]{:S(2)}, u32[]{:S(2)}) collective-permute-start(f32[64,512]{1,0:T(8,128)S(1)} %collective-permute-done.11.refs_15_.refs_6_), channel_id=1, source_target_pairs={{0,1},{1,0},{2,3},{3,2},{4,5},{5,4},{6,7},{7,6},{8,9},{9,8},{10,11... | collective-permute-start | bytes 393224 | tf_op jit(solution)/shard_map/ppermute | solution.py:218
  46.6 3.4 %collective-permute-done.10.refs_13_.refs_4_ = f32[64,512]{1,0:T(8,128)S(1)} collective-permute-done((f32[64,512]{1,0:T(8,128)S(1)}, f32[64,512]{1,0:T(8,128)S(1)}, u32[]{:S(2)}, u32[]{:S(2)}) %collective-permute-start.10) | collective-permute-done | bytes 131104 | tf_op jit(solution)/shard_map/ppermute | solution.py:218
  50.1 1.5 %collective-permute-start.16 = (f32[64,512]{1,0:T(8,128)S(1)}, f32[64,512]{1,0:T(8,128)S(1)}, u32[]{:S(2)}, u32[]{:S(2)}) collective-permute-start(f32[64,512]{1,0:T(8,128)S(1)} %collective-permute-done.10.refs_13_.refs_4_), channel_id=1, source_target_pairs={{0,1},{1,0},{2,3},{3,2},{4,5},{5,4},{6,7},{7,6},{8,9},{9,8},{10,11... | collective-permute-start | bytes 393224 | tf_op jit(solution)/shard_map/ppermute | solution.py:218
  52.1 1.3 %collective-permute-start.1 = (f32[256,256]{1,0:T(8,128)S(1)}, f32[256,256]{1,0:T(8,128)S(1)}, u32[]{:S(2)}, u32[]{:S(2)}) collective-permute-start(f32[256,256]{1,0:T(8,128)S(1)} %get-tuple-element.21.old_ref), channel_id=1, source_target_pairs={{0,16},{1,17},{10,26},{11,27},{20,4},{21,5},{30,14},{31,15}} | collective-permute-start | bytes 786440 | tf_op jit(solution)/shard_map/ppermute | solution.py:218
  53.4 1.6 %collective-permute-done.16.refs_14_.refs_5_ = f32[64,512]{1,0:T(8,128)S(1)} collective-permute-done((f32[64,512]{1,0:T(8,128)S(1)}, f32[64,512]{1,0:T(8,128)S(1)}, u32[]{:S(2)}, u32[]{:S(2)}) %collective-permute-start.16) | collective-permute-done | bytes 131104 | tf_op jit(solution)/shard_map/ppermute | solution.py:218
  55.0 1.5 %collective-permute-done.15.refs_12_.refs_3_ = f32[64,512]{1,0:T(8,128)S(1)} collective-permute-done((f32[64,512]{1,0:T(8,128)S(1)}, f32[64,512]{1,0:T(8,128)S(1)}, u32[]{:S(2)}, u32[]{:S(2)}) %collective-permute-start.15) | collective-permute-done | bytes 131104 | tf_op jit(solution)/shard_map/ppermute | solution.py:218
  56.5 0.9 shard_map.56
  57.5 1.8 %collective-permute-start.13 = (f32[256,256]{1,0:T(8,128)S(1)}, f32[256,256]{1,0:T(8,128)S(1)}, u32[]{:S(2)}, u32[]{:S(2)}) collective-permute-start(f32[256,256]{1,0:T(8,128)S(1)} %get-tuple-element.31), channel_id=1, source_target_pairs={{0,1},{1,0},{2,9},{3,8},{4,17},{5,16},{6,25},{7,24},{8,3},{9,2},{1... | collective-permute-start | bytes 786440 | tf_op jit(solution)/shard_map/ppermute | solution.py:218
  59.3 1.0 %collective-permute-done.1.got_ref = f32[256,256]{1,0:T(8,128)S(1)} collective-permute-done((f32[256,256]{1,0:T(8,128)S(1)}, f32[256,256]{1,0:T(8,128)S(1)}, u32[]{:S(2)}, u32[]{:S(2)}) %collective-permute-start.1) | collective-permute-done | bytes 262176 | tf_op jit(solution)/shard_map/ppermute | solution.py:218
  60.4 3.5 %collective-permute-start.2 = (f32[256,256]{1,0:T(8,128)S(1)}, f32[256,256]{1,0:T(8,128)S(1)}, u32[]{:S(2)}, u32[]{:S(2)}) collective-permute-start(f32[256,256]{1,0:T(8,128)S(1)} %shard_map.51.old_ref), channel_id=1, source_target_pairs={{0,8},{1,9},{4,12},{5,13},{10,2},{11,3},{14,6},{15,7},{16,24},{17,... | collective-permute-start | bytes 786440 | tf_op jit(solution)/shard_map/ppermute | solution.py:218
  63.9 2.9 %collective-permute-start.12 = (f32[256,256]{1,0:T(8,128)S(1)}, f32[256,256]{1,0:T(8,128)S(1)}, u32[]{:S(2)}, u32[]{:S(2)}) collective-permute-start(f32[256,256]{1,0:T(8,128)S(1)} %get-tuple-element.29), channel_id=1, source_target_pairs={{0,0},{1,1},{2,8},{3,9},{4,16},{5,17},{6,24},{7,25},{8,2},{9,3},{1... | collective-permute-start | bytes 786440 | tf_op jit(solution)/shard_map/ppermute | solution.py:218
  67.0 7.3 %collective-permute-done.19.got_ref = f32[128,256]{1,0:T(8,128)S(1)} collective-permute-done((f32[128,256]{1,0:T(8,128)S(1)}, f32[128,256]{1,0:T(8,128)S(1)}, u32[]{:S(2)}, u32[]{:S(2)}) %collective-permute-start.19) | collective-permute-done | bytes 131104 | tf_op jit(solution)/shard_map/ppermute | solution.py:218
  74.3 1.9 %collective-permute-start.20 = (f32[64,256]{1,0:T(8,128)S(1)}, f32[64,256]{1,0:T(8,128)S(1)}, u32[]{:S(2)}, u32[]{:S(2)}) collective-permute-start(f32[64,256]{1,0:T(8,128)S(1)} %get-tuple-element.36), channel_id=1, source_target_pairs={{0,0},{1,1},{2,8},{3,9},{4,16},{5,17},{6,24},{7,25},{8,4},{9,5},{1... | collective-permute-start | bytes 196616 | tf_op jit(solution)/shard_map/ppermute | solution.py:218
  76.3 0.8 collective-permute-start.21
  77.1 3.6 %collective-permute-done.13.refs_8_ = f32[256,256]{1,0:T(8,128)S(1)} collective-permute-done((f32[256,256]{1,0:T(8,128)S(1)}, f32[256,256]{1,0:T(8,128)S(1)}, u32[]{:S(2)}, u32[]{:S(2)}) %collective-permute-start.13) | collective-permute-done | bytes 262176 | tf_op jit(solution)/shard_map/ppermute | solution.py:218
  80.7 7.0 %collective-permute-done.12.refs_7_ = f32[256,256]{1,0:T(8,128)S(1)} collective-permute-done((f32[256,256]{1,0:T(8,128)S(1)}, f32[256,256]{1,0:T(8,128)S(1)}, u32[]{:S(2)}, u32[]{:S(2)}) %collective-permute-start.12) | collective-permute-done | bytes 262176 | tf_op jit(solution)/shard_map/ppermute | solution.py:218
  87.7 1.9 %shard_map.55 = f32[512,256]{1,0:T(8,128)} custom-call(f32[512,256]{1,0:T(8,128)S(1)} %copy-done.1, f32[512,256]{1,0:T(8,128)S(1)} %copy-done.2, f32[256,256]{1,0:T(8,128)S(1)} %shard_map.52.refs_2_, f32[256,512]{1,0:T(8,128)S(1)} %constant_dynamic-slice_fusion.refs_4_.refs_3_, f32[256,512]{1,0:T(8,128)S(1)} %collective-permute-done.3.refs_5_.refs_4_, ...), custom_call_target="tpu_custom_call" | custom-call | flops 603979776 | bytes 5505024 | tf_op jit(solution)/shard_map/pallas_call | solution.py:50
  89.5 0.7 shard_map.59
  (29 shorter events, 1.6 us)
Async XLA Ops:
  0.6 1.2 %copy-start = (f32[512,512]{1,0:T(8,128)S(1)}, f32[512,512]{1,0:T(8,128)}, u32[]{:S(2)}) copy-start(f32[512,512]{1,0:T(8,128)} %param.4) | copy-start | bytes 3145732
  1.9 13.8 %copy-start.1 = (f32[512,256]{1,0:T(8,128)S(1)}, f32[512,256]{1,0:T(8,128)}, u32[]{:S(2)}) copy-start(f32[512,256]{1,0:T(8,128)} %refs_8_.1) | copy-start | bytes 1572868
  1.9 13.8 %copy-start.2 = (f32[512,256]{1,0:T(8,128)S(1)}, f32[512,256]{1,0:T(8,128)}, u32[]{:S(2)}) copy-start(f32[512,256]{1,0:T(8,128)} %refs_1_.3) | copy-start | bytes 1572868
  1.9 13.7 %collective-permute-start = (f32[256,512]{1,0:T(8,128)S(1)}, f32[256,512]{1,0:T(8,128)S(1)}, u32[]{:S(2)}, u32[]{:S(2)}) collective-permute-start(f32[256,512]{1,0:T(8,128)S(1)} %constant_dynamic-slice_fusion.refs_4_.refs_3_), channel_id=1, source_target_pairs={{0,16},{1,17},{2,18},{3,19},{4,20},{5,21},{6,22},{7,23},{8,24},{9,... | collective-permute-start | bytes 1572872 | tf_op jit(solution)/shard_map/ppermute | solution.py:218
  2.0 29.1 %collective-permute-start.3 = (f32[256,512]{1,0:T(8,128)S(1)}, f32[256,512]{1,0:T(8,128)S(1)}, u32[]{:S(2)}, u32[]{:S(2)}) collective-permute-start(f32[256,512]{1,0:T(8,128)S(1)} %constant_dynamic-slice_fusion.refs_4_.refs_3_), channel_id=1, source_target_pairs={{0,8},{1,9},{2,10},{3,11},{4,12},{5,13},{6,14},{7,15},{8,0},{9,1},... | collective-permute-start | bytes 1572872 | tf_op jit(solution)/shard_map/ppermute | solution.py:218
  15.6 15.4 %collective-permute-start.4 = (f32[256,512]{1,0:T(8,128)S(1)}, f32[256,512]{1,0:T(8,128)S(1)}, u32[]{:S(2)}, u32[]{:S(2)}) collective-permute-start(f32[256,512]{1,0:T(8,128)S(1)} %collective-permute-done.refs_6_.refs_5_), channel_id=1, source_target_pairs={{0,8},{1,9},{2,10},{3,11},{4,12},{5,13},{6,14},{7,15},{8,0},{9,1},... | collective-permute-start | bytes 1572872 | tf_op jit(solution)/shard_map/ppermute | solution.py:218
  16.5 8.2 %collective-permute-start.5 = (f32[128,256]{1,0:T(8,128)S(1)}, f32[128,256]{1,0:T(8,128)S(1)}, u32[]{:S(2)}, u32[]{:S(2)}) collective-permute-start(f32[128,256]{1,0:T(8,128)S(1)} %get-tuple-element.24), channel_id=1, source_target_pairs={{0,2},{1,3},{2,0},{3,1},{4,6},{5,7},{6,4},{7,5},{8,10},{9,11},{10,... | collective-permute-start | bytes 393224 | tf_op jit(solution)/shard_map/ppermute | solution.py:218
  18.1 12.9 %collective-permute-start.6 = (f32[128,256]{1,0:T(8,128)S(1)}, f32[128,256]{1,0:T(8,128)S(1)}, u32[]{:S(2)}, u32[]{:S(2)}) collective-permute-start(f32[128,256]{1,0:T(8,128)S(1)} %get-tuple-element.25), channel_id=1, source_target_pairs={{0,4},{1,5},{2,6},{3,7},{4,0},{5,1},{6,2},{7,3},{8,12},{9,13},{10,... | collective-permute-start | bytes 393224 | tf_op jit(solution)/shard_map/ppermute | solution.py:218
  20.7 10.3 %collective-permute-start.7 = (f32[128,256]{1,0:T(8,128)S(1)}, f32[128,256]{1,0:T(8,128)S(1)}, u32[]{:S(2)}, u32[]{:S(2)}) collective-permute-start(f32[128,256]{1,0:T(8,128)S(1)} %get-tuple-element.26), channel_id=1, source_target_pairs={{0,6},{1,7},{2,4},{3,5},{4,2},{5,3},{6,0},{7,1},{8,14},{9,15},{10,... | collective-permute-start | bytes 393224 | tf_op jit(solution)/shard_map/ppermute | solution.py:218
  31.8 5.0 %collective-permute-start.8 = (f32[64,512]{1,0:T(8,128)S(1)}, f32[64,512]{1,0:T(8,128)S(1)}, u32[]{:S(2)}, u32[]{:S(2)}) collective-permute-start(f32[64,512]{1,0:T(8,128)S(1)} %get-tuple-element.28), channel_id=1, source_target_pairs={{0,1},{1,0},{2,3},{3,2},{4,5},{5,4},{6,7},{7,6},{8,9},{9,8},{10,11... | collective-permute-start | bytes 393224 | tf_op jit(solution)/shard_map/ppermute | solution.py:218
  36.9 8.3 %collective-permute-start.11 = (f32[64,512]{1,0:T(8,128)S(1)}, f32[64,512]{1,0:T(8,128)S(1)}, u32[]{:S(2)}, u32[]{:S(2)}) collective-permute-start(f32[64,512]{1,0:T(8,128)S(1)} %shard_map.54.refs_9_.refs_0_), channel_id=1, source_target_pairs={{0,6},{1,7},{2,4},{3,5},{4,2},{5,3},{6,0},{7,1},{8,14},{9,15},{10,... | collective-permute-start | bytes 393224 | tf_op jit(solution)/shard_map/ppermute | solution.py:218
  39.4 10.7 %collective-permute-start.10 = (f32[64,512]{1,0:T(8,128)S(1)}, f32[64,512]{1,0:T(8,128)S(1)}, u32[]{:S(2)}, u32[]{:S(2)}) collective-permute-start(f32[64,512]{1,0:T(8,128)S(1)} %shard_map.54.refs_9_.refs_0_), channel_id=1, source_target_pairs={{0,4},{1,5},{2,6},{3,7},{4,0},{5,1},{6,2},{7,3},{8,12},{9,13},{10,... | collective-permute-start | bytes 393224 | tf_op jit(solution)/shard_map/ppermute | solution.py:218
  41.0 10.6 %collective-permute-start.9 = (f32[64,512]{1,0:T(8,128)S(1)}, f32[64,512]{1,0:T(8,128)S(1)}, u32[]{:S(2)}, u32[]{:S(2)}) collective-permute-start(f32[64,512]{1,0:T(8,128)S(1)} %shard_map.54.refs_9_.refs_0_), channel_id=1, source_target_pairs={{0,2},{1,3},{2,0},{3,1},{4,6},{5,7},{6,4},{7,5},{8,10},{9,11},{10,... | collective-permute-start | bytes 393224 | tf_op jit(solution)/shard_map/ppermute | solution.py:218
  41.3 12.1 %collective-permute-start.14 = (f32[64,512]{1,0:T(8,128)S(1)}, f32[64,512]{1,0:T(8,128)S(1)}, u32[]{:S(2)}, u32[]{:S(2)}) collective-permute-start(f32[64,512]{1,0:T(8,128)S(1)} %shard_map.54.refs_9_.refs_0_), channel_id=1, source_target_pairs={{0,1},{1,0},{2,3},{3,2},{4,5},{5,4},{6,7},{7,6},{8,9},{9,8},{10,11... | collective-permute-start | bytes 393224 | tf_op jit(solution)/shard_map/ppermute | solution.py:218
  45.1 8.3 %collective-permute-start.17 = (f32[64,512]{1,0:T(8,128)S(1)}, f32[64,512]{1,0:T(8,128)S(1)}, u32[]{:S(2)}, u32[]{:S(2)}) collective-permute-start(f32[64,512]{1,0:T(8,128)S(1)} %collective-permute-done.11.refs_15_.refs_6_), channel_id=1, source_target_pairs={{0,1},{1,0},{2,3},{3,2},{4,5},{5,4},{6,7},{7,6},{8,9},{9,8},{10,11... | collective-permute-start | bytes 393224 | tf_op jit(solution)/shard_map/ppermute | solution.py:218
  50.1 5.0 %collective-permute-start.16 = (f32[64,512]{1,0:T(8,128)S(1)}, f32[64,512]{1,0:T(8,128)S(1)}, u32[]{:S(2)}, u32[]{:S(2)}) collective-permute-start(f32[64,512]{1,0:T(8,128)S(1)} %collective-permute-done.10.refs_13_.refs_4_), channel_id=1, source_target_pairs={{0,1},{1,0},{2,3},{3,2},{4,5},{5,4},{6,7},{7,6},{8,9},{9,8},{10,11... | collective-permute-start | bytes 393224 | tf_op jit(solution)/shard_map/ppermute | solution.py:218
  51.6 5.0 %collective-permute-start.15 = (f32[64,512]{1,0:T(8,128)S(1)}, f32[64,512]{1,0:T(8,128)S(1)}, u32[]{:S(2)}, u32[]{:S(2)}) collective-permute-start(f32[64,512]{1,0:T(8,128)S(1)} %collective-permute-done.9.refs_11_.refs_2_), channel_id=1, source_target_pairs={{0,1},{1,0},{2,3},{3,2},{4,5},{5,4},{6,7},{7,6},{8,9},{9,8},{10,11... | collective-permute-start | bytes 393224 | tf_op jit(solution)/shard_map/ppermute | solution.py:218
  52.1 8.3 %collective-permute-start.1 = (f32[256,256]{1,0:T(8,128)S(1)}, f32[256,256]{1,0:T(8,128)S(1)}, u32[]{:S(2)}, u32[]{:S(2)}) collective-permute-start(f32[256,256]{1,0:T(8,128)S(1)} %get-tuple-element.21.old_ref), channel_id=1, source_target_pairs={{0,16},{1,17},{10,26},{11,27},{20,4},{21,5},{30,14},{31,15}} | collective-permute-start | bytes 786440 | tf_op jit(solution)/shard_map/ppermute | solution.py:218
  57.4 9.4 %collective-permute-start.18 = (f32[256,256]{1,0:T(8,128)S(1)}, f32[256,256]{1,0:T(8,128)S(1)}, u32[]{:S(2)}, u32[]{:S(2)}) collective-permute-start(f32[256,256]{1,0:T(8,128)S(1)} %get-tuple-element.33), channel_id=1, source_target_pairs={{0,8},{1,9},{2,10},{3,11},{4,12},{5,13},{6,14},{7,15},{8,0},{9,1},... | collective-permute-start | bytes 786440 | tf_op jit(solution)/shard_map/ppermute | solution.py:218
  57.5 23.2 %collective-permute-start.13 = (f32[256,256]{1,0:T(8,128)S(1)}, f32[256,256]{1,0:T(8,128)S(1)}, u32[]{:S(2)}, u32[]{:S(2)}) collective-permute-start(f32[256,256]{1,0:T(8,128)S(1)} %get-tuple-element.31), channel_id=1, source_target_pairs={{0,1},{1,0},{2,9},{3,8},{4,17},{5,16},{6,25},{7,24},{8,3},{9,2},{1... | collective-permute-start | bytes 786440 | tf_op jit(solution)/shard_map/ppermute | solution.py:218
  60.4 16.7 %collective-permute-start.2 = (f32[256,256]{1,0:T(8,128)S(1)}, f32[256,256]{1,0:T(8,128)S(1)}, u32[]{:S(2)}, u32[]{:S(2)}) collective-permute-start(f32[256,256]{1,0:T(8,128)S(1)} %shard_map.51.old_ref), channel_id=1, source_target_pairs={{0,8},{1,9},{4,12},{5,13},{10,2},{11,3},{14,6},{15,7},{16,24},{17,... | collective-permute-start | bytes 786440 | tf_op jit(solution)/shard_map/ppermute | solution.py:218
  63.9 23.8 %collective-permute-start.12 = (f32[256,256]{1,0:T(8,128)S(1)}, f32[256,256]{1,0:T(8,128)S(1)}, u32[]{:S(2)}, u32[]{:S(2)}) collective-permute-start(f32[256,256]{1,0:T(8,128)S(1)} %get-tuple-element.29), channel_id=1, source_target_pairs={{0,0},{1,1},{2,8},{3,9},{4,16},{5,17},{6,24},{7,25},{8,2},{9,3},{1... | collective-permute-start | bytes 786440 | tf_op jit(solution)/shard_map/ppermute | solution.py:218
  66.9 7.4 %collective-permute-start.19 = (f32[128,256]{1,0:T(8,128)S(1)}, f32[128,256]{1,0:T(8,128)S(1)}, u32[]{:S(2)}, u32[]{:S(2)}) collective-permute-start(f32[128,256]{1,0:T(8,128)S(1)} %get-tuple-element.35), channel_id=1, source_target_pairs={{0,16},{1,17},{2,18},{3,19},{4,20},{5,21},{6,22},{7,23},{8,24},{9,... | collective-permute-start | bytes 393224 | tf_op jit(solution)/shard_map/ppermute | solution.py:218
  74.3 15.2 %collective-permute-start.20 = (f32[64,256]{1,0:T(8,128)S(1)}, f32[64,256]{1,0:T(8,128)S(1)}, u32[]{:S(2)}, u32[]{:S(2)}) collective-permute-start(f32[64,256]{1,0:T(8,128)S(1)} %get-tuple-element.36), channel_id=1, source_target_pairs={{0,0},{1,1},{2,8},{3,9},{4,16},{5,17},{6,24},{7,25},{8,4},{9,5},{1... | collective-permute-start | bytes 196616 | tf_op jit(solution)/shard_map/ppermute | solution.py:218
  76.3 13.3 %collective-permute-start.21 = (f32[64,256]{1,0:T(8,128)S(1)}, f32[64,256]{1,0:T(8,128)S(1)}, u32[]{:S(2)}, u32[]{:S(2)}) collective-permute-start(f32[64,256]{1,0:T(8,128)S(1)} %get-tuple-element.37), channel_id=1, source_target_pairs={{0,1},{1,0},{2,9},{3,8},{4,17},{5,16},{6,25},{7,24},{8,5},{9,4},{1... | collective-permute-start | bytes 196616 | tf_op jit(solution)/shard_map/ppermute | solution.py:218
where the time goes:
time: 90.4 us; the launch traced here: 90.2 us
  waiting for transfers between devices  55 us (61%)
  starting transfers between devices  28 us (31%)
  Pallas kernels  5.13 us (6%)
  local copies, waits for them, and re-layouts  1.25 us (1%)
    ppermute x22, waiting for transfers between devices, send(): return lax.ppermute(value, AXES, pairs)  55 us
    ppermute x22, starting transfers between devices, send(): return lax.ppermute(value, AXES, pairs)  28 us
    pallas_call x10, Pallas kernels, call(): pl.pallas_call(kernel, out_shape=outs, in_specs=[pl.BlockSpec(memory_spac...  5.13 us
  transfers between devices with their start and end apart: 22, of which 12 were waited for; matrix products, arithmetic and copies ran while one was open for 0% of the time, Pallas kernels for 4%

commit v1 on v0

--- a/solution.py
+++ b/solution.py
@@ -79,7 +79,7 @@
         copy.wait()
 
 
-def cut_rows(arrays, cuts, fold):
+def cut_rows(arrays, cuts, fold, grant):
     outs = [shape(rows, arrays[source].shape[1]) for source, rows, _ in cuts]
     return call(
         functools.partial(cut_kernel, cuts, fold),
@@ -87,6 +87,7 @@
         arrays,
         scratch=[pltpu.SemaphoreType.DMA((len(cuts),))],
         hbm=range(len(arrays)),
+        grant=grant,
     )
 
 
@@ -217,8 +218,8 @@
                         pairs.append((start, to[0] * col_count + to[1] * fold + to[2]))
         return lax.ppermute(value, AXES, pairs)
 
-    b = lax.axis_index("col") % fold
-    blocks = {0: lax.dynamic_slice_in_dim(features, b * own_cols, own_cols, 0)}
+    cuts = [(0, own_cols, lambda r, q, b: b)]
+    blocks = {0: cut_rows([features], cuts, fold, 63)[0]}
     for bit in reversed(bits):
         for t in list(blocks):
             blocks[t | bit] = send(blocks[t], lambda i, j, k: (i ^ bit, j, k))
@@ -227,14 +228,16 @@
     cuts = [(0, quarter, lambda r, q, b, s=s: q ^ s) for s in every]
     cuts += [(0, own_cols, lambda r, q, b, d=d: b ^ d) for d in both]
     cuts += [(1, own_cols, lambda r, q, b: b)]
-    cut = cut_rows([coeffs, factors], cuts, fold)
+    cut = cut_rows([coeffs, factors], cuts, fold, 2)
     parts, turns, col_factors = cut[:row_count], cut[row_count:-1], cut[-1]
     parts = [send(parts[s], lambda i, j, k: (i, j ^ s, k)) if s else parts[s] for s in every]
 
+    turns = [send(turns[d], lambda i, j, k: (i, j, k ^ d)) if d else turns[d] for d in both]
+
     def mirror(d, *deps):
-        return send(after(turns[d], *deps), lambda i, j, k: (j, i, k ^ d))
-
-    mirrored = {fold - 1: mirror(fold - 1, *parts)}
+        return send(after(turns[d], *deps), lambda i, j, k: (j, i, k))
+
+    mirrored = {0: mirror(0, *parts)}
 
     shares = call(
         functools.partial(residual_kernel, row_count, fold),
@@ -263,7 +266,7 @@
         for d in both:
             one = chunks[s]
             spread.append(send(one, lambda i, j, k: (i, j, k ^ d)) if d else one)
-    for d in range(fold - 1):
+    for d in range(1, fold):
         mirrored[d] = mirror(d, *chunks)
 
     halves = [pltpu.VMEM((own_rows, width), BF16)] * 2

time: 90.4 us -> 96.4 us (1.066)
  starting transfers between devices: 28 us -> 31 us
  Pallas kernels: 5.13 us -> 7 us
  waiting for transfers between devices: 55 us -> 56.2 us
    ppermute x22 -> x23, starting transfers between devices: 28 us -> 31 us  [send(): return lax.ppermute(value, AXES, pairs)]
    pallas_call x10 -> x11, Pallas kernels: 5.13 us -> 7 us  [call(): pl.pallas_call(kernel, out_shape=outs, in_specs=[pl.BlockSpec(memory_spac...]
    ppermute x22 -> x23, waiting for transfers between devices: 55 us -> 56.2 us  [send(): return lax.ppermute(value, AXES, pairs)]
  transfers between devices with their start and end apart: 22 -> 23, of which waited for: 12 -> 12; matrix products, arithmetic and copies ran while one was open for 0% -> 0% of each run, Pallas kernels for 4% -> 4%
where the time goes in v1:
time: 96.4 us; the launch traced here: 96.2 us
  waiting for transfers between devices  56.2 us (58%)
  starting transfers between devices  31 us (32%)
  Pallas kernels  7 us (7%)
  local copies, waits for them, and re-layouts  1.05 us (1%)
    ppermute x23, waiting for transfers between devices, send(): return lax.ppermute(value, AXES, pairs)  56.2 us
    ppermute x23, starting transfers between devices, send(): return lax.ppermute(value, AXES, pairs)  31 us
    pallas_call x11, Pallas kernels, call(): pl.pallas_call(kernel, out_shape=outs, in_specs=[pl.BlockSpec(memory_spac...  7 us
  transfers between devices with their start and end apart: 23, of which 12 were waited for; matrix products, arithmetic and copies ran while one was open for 0% of the time, Pallas kernels for 4%

profile of v1, /device:TPU:4, one launch (start us, length us, event | category | flops | bytes accessed | tf_op | source)
XLA Modules:
  0.0 96.2 jit_solution(8999719668393244138)
XLA Ops:
  0.6 1.9 %shard_map.51.refs_4_.refs_3_ = f32[256,512]{1,0:T(8,128)} custom-call(f32[512,512]{1,0:T(8,128)} %refs_0_.4), custom_call_target="tpu_custom_call" | custom-call | bytes 1572864 | tf_op jit(solution)/shard_map/pallas_call | solution.py:50
  2.7 13.8 %collective-permute-done.refs_6_.refs_5_ = f32[256,512]{1,0:T(8,128)S(1)} collective-permute-done((f32[256,512]{1,0:T(8,128)}, f32[256,512]{1,0:T(8,128)S(1)}, u32[]{:S(2)}, u32[]{:S(2)}) %collective-permute-start) | collective-permute-done | bytes 524320 | tf_op jit(solution)/shard_map/ppermute | solution.py:219
  16.5 1.0 %copy-done.2 = f32[512,256]{1,0:T(8,128)S(1)} copy-done((f32[512,256]{1,0:T(8,128)S(1)}, f32[512,256]{1,0:T(8,128)}, u32[]{:S(2)}) %copy-start.2) | copy-done | bytes 524312
  17.6 0.8 shard_map.50
  18.3 1.6 %collective-permute-start.5 = (f32[128,256]{1,0:T(8,128)S(1)}, f32[128,256]{1,0:T(8,128)S(1)}, u32[]{:S(2)}, u32[]{:S(2)}) collective-permute-start(f32[128,256]{1,0:T(8,128)S(1)} %get-tuple-element.24), channel_id=1, source_target_pairs={{0,2},{1,3},{2,0},{3,1},{4,6},{5,7},{6,4},{7,5},{8,10},{9,11},{10,... | collective-permute-start | bytes 393224 | tf_op jit(solution)/shard_map/ppermute | solution.py:219
  20.0 2.6 %collective-permute-start.6 = (f32[128,256]{1,0:T(8,128)S(1)}, f32[128,256]{1,0:T(8,128)S(1)}, u32[]{:S(2)}, u32[]{:S(2)}) collective-permute-start(f32[128,256]{1,0:T(8,128)S(1)} %get-tuple-element.25), channel_id=1, source_target_pairs={{0,4},{1,5},{2,6},{3,7},{4,0},{5,1},{6,2},{7,3},{8,12},{9,13},{10,... | collective-permute-start | bytes 393224 | tf_op jit(solution)/shard_map/ppermute | solution.py:219
  22.8 3.8 %collective-permute-done.5.refs_1_ = f32[128,256]{1,0:T(8,128)S(1)} collective-permute-done((f32[128,256]{1,0:T(8,128)S(1)}, f32[128,256]{1,0:T(8,128)S(1)}, u32[]{:S(2)}, u32[]{:S(2)}) %collective-permute-start.5) | collective-permute-done | bytes 131104 | tf_op jit(solution)/shard_map/ppermute | solution.py:219
  26.6 6.3 %collective-permute-done.6.refs_2_ = f32[128,256]{1,0:T(8,128)S(1)} collective-permute-done((f32[128,256]{1,0:T(8,128)S(1)}, f32[128,256]{1,0:T(8,128)S(1)}, u32[]{:S(2)}, u32[]{:S(2)}) %collective-permute-start.6) | collective-permute-done | bytes 131104 | tf_op jit(solution)/shard_map/ppermute | solution.py:219
  32.9 0.7 shard_map.54
  33.7 1.6 %collective-permute-start.10 = (f32[64,512]{1,0:T(8,128)S(1)}, f32[64,512]{1,0:T(8,128)S(1)}, u32[]{:S(2)}, u32[]{:S(2)}) collective-permute-start(f32[64,512]{1,0:T(8,128)S(1)} %get-tuple-element.30), channel_id=1, source_target_pairs={{0,1},{1,0},{2,3},{3,2},{4,5},{5,4},{6,7},{7,6},{8,9},{9,8},{10,11... | collective-permute-start | bytes 393224 | tf_op jit(solution)/shard_map/ppermute | solution.py:219
  35.2 3.5 %collective-permute-done.10.right = f32[64,512]{1,0:T(8,128)S(1)} collective-permute-done((f32[64,512]{1,0:T(8,128)S(1)}, f32[64,512]{1,0:T(8,128)S(1)}, u32[]{:S(2)}, u32[]{:S(2)}) %collective-permute-start.10) | collective-permute-done | bytes 131104 | tf_op jit(solution)/shard_map/ppermute | solution.py:219
  38.7 2.5 %collective-permute-start.13 = (f32[64,512]{1,0:T(8,128)S(1)}, f32[64,512]{1,0:T(8,128)S(1)}, u32[]{:S(2)}, u32[]{:S(2)}) collective-permute-start(f32[64,512]{1,0:T(8,128)S(1)} %shard_map.55.refs_9_.refs_0_), channel_id=1, source_target_pairs={{0,6},{1,7},{2,4},{3,5},{4,2},{5,3},{6,0},{7,1},{8,14},{9,15},{10,... | collective-permute-start | bytes 393224 | tf_op jit(solution)/shard_map/ppermute | solution.py:219
  41.3 1.6 %collective-permute-start.12 = (f32[64,512]{1,0:T(8,128)S(1)}, f32[64,512]{1,0:T(8,128)S(1)}, u32[]{:S(2)}, u32[]{:S(2)}) collective-permute-start(f32[64,512]{1,0:T(8,128)S(1)} %shard_map.55.refs_9_.refs_0_), channel_id=1, source_target_pairs={{0,4},{1,5},{2,6},{3,7},{4,0},{5,1},{6,2},{7,3},{8,12},{9,13},{10,... | collective-permute-start | bytes 393224 | tf_op jit(solution)/shard_map/ppermute | solution.py:219
  43.2 1.5 %collective-permute-start.15 = (f32[64,512]{1,0:T(8,128)S(1)}, f32[64,512]{1,0:T(8,128)S(1)}, u32[]{:S(2)}, u32[]{:S(2)}) collective-permute-start(f32[64,512]{1,0:T(8,128)S(1)} %shard_map.55.refs_9_.refs_0_), channel_id=1, source_target_pairs={{0,1},{1,0},{2,3},{3,2},{4,5},{5,4},{6,7},{7,6},{8,9},{9,8},{10,11... | collective-permute-start | bytes 393224 | tf_op jit(solution)/shard_map/ppermute | solution.py:219
  44.7 2.3 %collective-permute-done.13.refs_15_.refs_6_ = f32[64,512]{1,0:T(8,128)S(1)} collective-permute-done((f32[64,512]{1,0:T(8,128)S(1)}, f32[64,512]{1,0:T(8,128)S(1)}, u32[]{:S(2)}, u32[]{:S(2)}) %collective-permute-start.13) | collective-permute-done | bytes 131104 | tf_op jit(solution)/shard_map/ppermute | solution.py:219
  47.0 1.5 %collective-permute-start.18 = (f32[64,512]{1,0:T(8,128)S(1)}, f32[64,512]{1,0:T(8,128)S(1)}, u32[]{:S(2)}, u32[]{:S(2)}) collective-permute-start(f32[64,512]{1,0:T(8,128)S(1)} %collective-permute-done.13.refs_15_.refs_6_), channel_id=1, source_target_pairs={{0,1},{1,0},{2,3},{3,2},{4,5},{5,4},{6,7},{7,6},{8,9},{9,8},{10,11... | collective-permute-start | bytes 393224 | tf_op jit(solution)/shard_map/ppermute | solution.py:219
  48.5 3.5 %collective-permute-done.12.refs_13_.refs_4_ = f32[64,512]{1,0:T(8,128)S(1)} collective-permute-done((f32[64,512]{1,0:T(8,128)S(1)}, f32[64,512]{1,0:T(8,128)S(1)}, u32[]{:S(2)}, u32[]{:S(2)}) %collective-permute-start.12) | collective-permute-done | bytes 131104 | tf_op jit(solution)/shard_map/ppermute | solution.py:219
  52.0 1.5 %collective-permute-start.17 = (f32[64,512]{1,0:T(8,128)S(1)}, f32[64,512]{1,0:T(8,128)S(1)}, u32[]{:S(2)}, u32[]{:S(2)}) collective-permute-start(f32[64,512]{1,0:T(8,128)S(1)} %collective-permute-done.12.refs_13_.refs_4_), channel_id=1, source_target_pairs={{0,1},{1,0},{2,3},{3,2},{4,5},{5,4},{6,7},{7,6},{8,9},{9,8},{10,11... | collective-permute-start | bytes 393224 | tf_op jit(solution)/shard_map/ppermute | solution.py:219
  54.0 1.3 %collective-permute-start.1 = (f32[256,256]{1,0:T(8,128)S(1)}, f32[256,256]{1,0:T(8,128)S(1)}, u32[]{:S(2)}, u32[]{:S(2)}) collective-permute-start(f32[256,256]{1,0:T(8,128)S(1)} %get-tuple-element.21.old_ref), channel_id=1, source_target_pairs={{0,16},{1,17},{10,26},{11,27},{20,4},{21,5},{30,14},{31,15}} | collective-permute-start | bytes 786440 | tf_op jit(solution)/shard_map/ppermute | solution.py:219
  55.3 1.6 %collective-permute-start.9 = (f32[256,256]{1,0:T(8,128)S(1)}, f32[256,256]{1,0:T(8,128)S(1)}, u32[]{:S(2)}, u32[]{:S(2)}) collective-permute-start(f32[256,256]{1,0:T(8,128)S(1)} %get-tuple-element.28), channel_id=1, source_target_pairs={{0,1},{1,0},{2,3},{3,2},{4,5},{5,4},{6,7},{7,6},{8,9},{9,8},{10,11... | collective-permute-start | bytes 786440 | tf_op jit(solution)/shard_map/ppermute | solution.py:219
  56.9 1.5 %collective-permute-done.17.refs_14_.refs_5_ = f32[64,512]{1,0:T(8,128)S(1)} collective-permute-done((f32[64,512]{1,0:T(8,128)S(1)}, f32[64,512]{1,0:T(8,128)S(1)}, u32[]{:S(2)}, u32[]{:S(2)}) %collective-permute-start.17) | collective-permute-done | bytes 131104 | tf_op jit(solution)/shard_map/ppermute | solution.py:219
  58.4 2.7 %collective-permute-done.16.refs_12_.refs_3_ = f32[64,512]{1,0:T(8,128)S(1)} collective-permute-done((f32[64,512]{1,0:T(8,128)S(1)}, f32[64,512]{1,0:T(8,128)S(1)}, u32[]{:S(2)}, u32[]{:S(2)}) %collective-permute-start.16) | collective-permute-done | bytes 131104 | tf_op jit(solution)/shard_map/ppermute | solution.py:219
  61.0 0.9 shard_map.57
  62.0 3.1 %collective-permute-start.8 = (f32[256,256]{1,0:T(8,128)S(1)}, f32[256,256]{1,0:T(8,128)S(1)}, u32[]{:S(2)}, u32[]{:S(2)}) collective-permute-start(f32[256,256]{1,0:T(8,128)S(1)} %get-tuple-element.27), channel_id=1, source_target_pairs={{0,0},{1,1},{2,8},{3,9},{4,16},{5,17},{6,24},{7,25},{8,2},{9,3},{1... | collective-permute-start | bytes 786440 | tf_op jit(solution)/shard_map/ppermute | solution.py:219
  65.2 3.3 %collective-permute-start.2 = (f32[256,256]{1,0:T(8,128)S(1)}, f32[256,256]{1,0:T(8,128)S(1)}, u32[]{:S(2)}, u32[]{:S(2)}) collective-permute-start(f32[256,256]{1,0:T(8,128)S(1)} %shard_map.52.old_ref), channel_id=1, source_target_pairs={{0,8},{1,9},{4,12},{5,13},{10,2},{11,3},{14,6},{15,7},{16,24},{17,... | collective-permute-start | bytes 786440 | tf_op jit(solution)/shard_map/ppermute | solution.py:219
  68.5 3.9 %collective-permute-start.14 = (f32[256,256]{1,0:T(8,128)S(1)}, f32[256,256]{1,0:T(8,128)S(1)}, u32[]{:S(2)}, u32[]{:S(2)}) collective-permute-start(f32[256,256]{1,0:T(8,128)S(1)} %collective-permute-done.9), channel_id=1, source_target_pairs={{0,0},{1,1},{2,8},{3,9},{4,16},{5,17},{6,24},{7,25},{8,2},{9,3},{1... | collective-permute-start | bytes 786440 | tf_op jit(solution)/shard_map/ppermute | solution.py:219
  72.6 7.9 %collective-permute-done.20.got_ref = f32[128,256]{1,0:T(8,128)S(1)} collective-permute-done((f32[128,256]{1,0:T(8,128)S(1)}, f32[128,256]{1,0:T(8,128)S(1)}, u32[]{:S(2)}, u32[]{:S(2)}) %collective-permute-start.20) | collective-permute-done | bytes 131104 | tf_op jit(solution)/shard_map/ppermute | solution.py:219
  80.5 2.1 %collective-permute-start.21 = (f32[64,256]{1,0:T(8,128)S(1)}, f32[64,256]{1,0:T(8,128)S(1)}, u32[]{:S(2)}, u32[]{:S(2)}) collective-permute-start(f32[64,256]{1,0:T(8,128)S(1)} %get-tuple-element.36), channel_id=1, source_target_pairs={{0,0},{1,1},{2,8},{3,9},{4,16},{5,17},{6,24},{7,25},{8,4},{9,5},{1... | collective-permute-start | bytes 196616 | tf_op jit(solution)/shard_map/ppermute | solution.py:219
  82.7 3.4 %collective-permute-done.8.refs_7_ = f32[256,256]{1,0:T(8,128)S(1)} collective-permute-done((f32[256,256]{1,0:T(8,128)S(1)}, f32[256,256]{1,0:T(8,128)S(1)}, u32[]{:S(2)}, u32[]{:S(2)}) %collective-permute-start.8) | collective-permute-done | bytes 262176 | tf_op jit(solution)/shard_map/ppermute | solution.py:219
  86.1 7.0 %collective-permute-done.14.refs_8_ = f32[256,256]{1,0:T(8,128)S(1)} collective-permute-done((f32[256,256]{1,0:T(8,128)S(1)}, f32[256,256]{1,0:T(8,128)S(1)}, u32[]{:S(2)}, u32[]{:S(2)}) %collective-permute-start.14) | collective-permute-done | bytes 262176 | tf_op jit(solution)/shard_map/ppermute | solution.py:219
  93.1 1.9 %shard_map.56 = f32[512,256]{1,0:T(8,128)} custom-call(f32[512,256]{1,0:T(8,128)S(1)} %copy-done.1, f32[512,256]{1,0:T(8,128)S(1)} %copy-done.3, f32[256,256]{1,0:T(8,128)S(1)} %shard_map.53.refs_2_, f32[256,512]{1,0:T(8,128)S(1)} %copy-done, f32[256,512]{1,0:T(8,128)S(1)} %collective-permute-done.3.refs_5_.refs_4_, ...), custom_call_target="tpu_custom_call" | custom-call | flops 603979776 | bytes 5505024 | tf_op jit(solution)/shard_map/pallas_call | solution.py:50
  95.5 0.7 shard_map.60
  (33 shorter events, 2.1 us)
Async XLA Ops:
  0.6 15.9 %copy-start.1 = (f32[512,256]{1,0:T(8,128)S(1)}, f32[512,256]{1,0:T(8,128)}, u32[]{:S(2)}) copy-start(f32[512,256]{1,0:T(8,128)} %refs_8_.1) | copy-start | bytes 1572868
  2.6 30.4 %copy-start = (f32[256,512]{1,0:T(8,128)S(1)}, f32[256,512]{1,0:T(8,128)}, u32[]{:S(2)}) copy-start(f32[256,512]{1,0:T(8,128)} %shard_map.51.refs_4_.refs_3_) | copy-start | bytes 1572868
  2.6 13.9 %collective-permute-start = (f32[256,512]{1,0:T(8,128)}, f32[256,512]{1,0:T(8,128)S(1)}, u32[]{:S(2)}, u32[]{:S(2)}) collective-permute-start(f32[256,512]{1,0:T(8,128)} %shard_map.51.refs_4_.refs_3_), channel_id=1, source_target_pairs={{0,16},{1,17},{2,18},{3,19},{4,20},{5,21},{6,22},{7,23},{8,24},{9,... | collective-permute-start | bytes 1572872 | tf_op jit(solution)/shard_map/ppermute | solution.py:219
  2.6 30.3 %collective-permute-start.3 = (f32[256,512]{1,0:T(8,128)}, f32[256,512]{1,0:T(8,128)S(1)}, u32[]{:S(2)}, u32[]{:S(2)}) collective-permute-start(f32[256,512]{1,0:T(8,128)} %shard_map.51.refs_4_.refs_3_), channel_id=1, source_target_pairs={{0,8},{1,9},{2,10},{3,11},{4,12},{5,13},{6,14},{7,15},{8,0},{9,1},... | collective-permute-start | bytes 1572872 | tf_op jit(solution)/shard_map/ppermute | solution.py:219
  16.5 16.4 %collective-permute-start.4 = (f32[256,512]{1,0:T(8,128)S(1)}, f32[256,512]{1,0:T(8,128)S(1)}, u32[]{:S(2)}, u32[]{:S(2)}) collective-permute-start(f32[256,512]{1,0:T(8,128)S(1)} %collective-permute-done.refs_6_.refs_5_), channel_id=1, source_target_pairs={{0,8},{1,9},{2,10},{3,11},{4,12},{5,13},{6,14},{7,15},{8,0},{9,1},... | collective-permute-start | bytes 1572872 | tf_op jit(solution)/shard_map/ppermute | solution.py:219
  16.5 1.0 %copy-start.2 = (f32[512,256]{1,0:T(8,128)S(1)}, f32[512,256]{1,0:T(8,128)}, u32[]{:S(2)}) copy-start(f32[512,256]{1,0:T(8,128)} %refs_1_.3) | copy-start | bytes 1572868
  18.3 8.3 %collective-permute-start.5 = (f32[128,256]{1,0:T(8,128)S(1)}, f32[128,256]{1,0:T(8,128)S(1)}, u32[]{:S(2)}, u32[]{:S(2)}) collective-permute-start(f32[128,256]{1,0:T(8,128)S(1)} %get-tuple-element.24), channel_id=1, source_target_pairs={{0,2},{1,3},{2,0},{3,1},{4,6},{5,7},{6,4},{7,5},{8,10},{9,11},{10,... | collective-permute-start | bytes 393224 | tf_op jit(solution)/shard_map/ppermute | solution.py:219
  20.0 12.9 %collective-permute-start.6 = (f32[128,256]{1,0:T(8,128)S(1)}, f32[128,256]{1,0:T(8,128)S(1)}, u32[]{:S(2)}, u32[]{:S(2)}) collective-permute-start(f32[128,256]{1,0:T(8,128)S(1)} %get-tuple-element.25), channel_id=1, source_target_pairs={{0,4},{1,5},{2,6},{3,7},{4,0},{5,1},{6,2},{7,3},{8,12},{9,13},{10,... | collective-permute-start | bytes 393224 | tf_op jit(solution)/shard_map/ppermute | solution.py:219
  22.6 10.3 %collective-permute-start.7 = (f32[128,256]{1,0:T(8,128)S(1)}, f32[128,256]{1,0:T(8,128)S(1)}, u32[]{:S(2)}, u32[]{:S(2)}) collective-permute-start(f32[128,256]{1,0:T(8,128)S(1)} %get-tuple-element.26), channel_id=1, source_target_pairs={{0,6},{1,7},{2,4},{3,5},{4,2},{5,3},{6,0},{7,1},{8,14},{9,15},{10,... | collective-permute-start | bytes 393224 | tf_op jit(solution)/shard_map/ppermute | solution.py:219
  33.7 5.0 %collective-permute-start.10 = (f32[64,512]{1,0:T(8,128)S(1)}, f32[64,512]{1,0:T(8,128)S(1)}, u32[]{:S(2)}, u32[]{:S(2)}) collective-permute-start(f32[64,512]{1,0:T(8,128)S(1)} %get-tuple-element.30), channel_id=1, source_target_pairs={{0,1},{1,0},{2,3},{3,2},{4,5},{5,4},{6,7},{7,6},{8,9},{9,8},{10,11... | collective-permute-start | bytes 393224 | tf_op jit(solution)/shard_map/ppermute | solution.py:219
  38.7 8.3 %collective-permute-start.13 = (f32[64,512]{1,0:T(8,128)S(1)}, f32[64,512]{1,0:T(8,128)S(1)}, u32[]{:S(2)}, u32[]{:S(2)}) collective-permute-start(f32[64,512]{1,0:T(8,128)S(1)} %shard_map.55.refs_9_.refs_0_), channel_id=1, source_target_pairs={{0,6},{1,7},{2,4},{3,5},{4,2},{5,3},{6,0},{7,1},{8,14},{9,15},{10,... | collective-permute-start | bytes 393224 | tf_op jit(solution)/shard_map/ppermute | solution.py:219
  41.3 10.7 %collective-permute-start.12 = (f32[64,512]{1,0:T(8,128)S(1)}, f32[64,512]{1,0:T(8,128)S(1)}, u32[]{:S(2)}, u32[]{:S(2)}) collective-permute-start(f32[64,512]{1,0:T(8,128)S(1)} %shard_map.55.refs_9_.refs_0_), channel_id=1, source_target_pairs={{0,4},{1,5},{2,6},{3,7},{4,0},{5,1},{6,2},{7,3},{8,12},{9,13},{10,... | collective-permute-start | bytes 393224 | tf_op jit(solution)/shard_map/ppermute | solution.py:219
  42.9 10.6 %collective-permute-start.11 = (f32[64,512]{1,0:T(8,128)S(1)}, f32[64,512]{1,0:T(8,128)S(1)}, u32[]{:S(2)}, u32[]{:S(2)}) collective-permute-start(f32[64,512]{1,0:T(8,128)S(1)} %shard_map.55.refs_9_.refs_0_), channel_id=1, source_target_pairs={{0,2},{1,3},{2,0},{3,1},{4,6},{5,7},{6,4},{7,5},{8,10},{9,11},{10,... | collective-permute-start | bytes 393224 | tf_op jit(solution)/shard_map/ppermute | solution.py:219
  43.2 12.1 %collective-permute-start.15 = (f32[64,512]{1,0:T(8,128)S(1)}, f32[64,512]{1,0:T(8,128)S(1)}, u32[]{:S(2)}, u32[]{:S(2)}) collective-permute-start(f32[64,512]{1,0:T(8,128)S(1)} %shard_map.55.refs_9_.refs_0_), channel_id=1, source_target_pairs={{0,1},{1,0},{2,3},{3,2},{4,5},{5,4},{6,7},{7,6},{8,9},{9,8},{10,11... | collective-permute-start | bytes 393224 | tf_op jit(solution)/shard_map/ppermute | solution.py:219
  47.0 9.9 %collective-permute-start.18 = (f32[64,512]{1,0:T(8,128)S(1)}, f32[64,512]{1,0:T(8,128)S(1)}, u32[]{:S(2)}, u32[]{:S(2)}) collective-permute-start(f32[64,512]{1,0:T(8,128)S(1)} %collective-permute-done.13.refs_15_.refs_6_), channel_id=1, source_target_pairs={{0,1},{1,0},{2,3},{3,2},{4,5},{5,4},{6,7},{7,6},{8,9},{9,8},{10,11... | collective-permute-start | bytes 393224 | tf_op jit(solution)/shard_map/ppermute | solution.py:219
  52.0 6.4 %collective-permute-start.17 = (f32[64,512]{1,0:T(8,128)S(1)}, f32[64,512]{1,0:T(8,128)S(1)}, u32[]{:S(2)}, u32[]{:S(2)}) collective-permute-start(f32[64,512]{1,0:T(8,128)S(1)} %collective-permute-done.12.refs_13_.refs_4_), channel_id=1, source_target_pairs={{0,1},{1,0},{2,3},{3,2},{4,5},{5,4},{6,7},{7,6},{8,9},{9,8},{10,11... | collective-permute-start | bytes 393224 | tf_op jit(solution)/shard_map/ppermute | solution.py:219
  53.5 7.5 %collective-permute-start.16 = (f32[64,512]{1,0:T(8,128)S(1)}, f32[64,512]{1,0:T(8,128)S(1)}, u32[]{:S(2)}, u32[]{:S(2)}) collective-permute-start(f32[64,512]{1,0:T(8,128)S(1)} %collective-permute-done.11.refs_11_.refs_2_), channel_id=1, source_target_pairs={{0,1},{1,0},{2,3},{3,2},{4,5},{5,4},{6,7},{7,6},{8,9},{9,8},{10,11... | collective-permute-start | bytes 393224 | tf_op jit(solution)/shard_map/ppermute | solution.py:219
  54.0 11.1 %collective-permute-start.1 = (f32[256,256]{1,0:T(8,128)S(1)}, f32[256,256]{1,0:T(8,128)S(1)}, u32[]{:S(2)}, u32[]{:S(2)}) collective-permute-start(f32[256,256]{1,0:T(8,128)S(1)} %get-tuple-element.21.old_ref), channel_id=1, source_target_pairs={{0,16},{1,17},{10,26},{11,27},{20,4},{21,5},{30,14},{31,15}} | collective-permute-start | bytes 786440 | tf_op jit(solution)/shard_map/ppermute | solution.py:219
  55.3 13.2 %collective-permute-start.9 = (f32[256,256]{1,0:T(8,128)S(1)}, f32[256,256]{1,0:T(8,128)S(1)}, u32[]{:S(2)}, u32[]{:S(2)}) collective-permute-start(f32[256,256]{1,0:T(8,128)S(1)} %get-tuple-element.28), channel_id=1, source_target_pairs={{0,1},{1,0},{2,3},{3,2},{4,5},{5,4},{6,7},{7,6},{8,9},{9,8},{10,11... | collective-permute-start | bytes 786440 | tf_op jit(solution)/shard_map/ppermute | solution.py:219
  61.9 10.5 %collective-permute-start.19 = (f32[256,256]{1,0:T(8,128)S(1)}, f32[256,256]{1,0:T(8,128)S(1)}, u32[]{:S(2)}, u32[]{:S(2)}) collective-permute-start(f32[256,256]{1,0:T(8,128)S(1)} %get-tuple-element.33), channel_id=1, source_target_pairs={{0,8},{1,9},{2,10},{3,11},{4,12},{5,13},{6,14},{7,15},{8,0},{9,1},... | collective-permute-start | bytes 786440 | tf_op jit(solution)/shard_map/ppermute | solution.py:219
  62.0 24.0 %collective-permute-start.8 = (f32[256,256]{1,0:T(8,128)S(1)}, f32[256,256]{1,0:T(8,128)S(1)}, u32[]{:S(2)}, u32[]{:S(2)}) collective-permute-start(f32[256,256]{1,0:T(8,128)S(1)} %get-tuple-element.27), channel_id=1, source_target_pairs={{0,0},{1,1},{2,8},{3,9},{4,16},{5,17},{6,24},{7,25},{8,2},{9,3},{1... | collective-permute-start | bytes 786440 | tf_op jit(solution)/shard_map/ppermute | solution.py:219
  65.2 17.5 %collective-permute-start.2 = (f32[256,256]{1,0:T(8,128)S(1)}, f32[256,256]{1,0:T(8,128)S(1)}, u32[]{:S(2)}, u32[]{:S(2)}) collective-permute-start(f32[256,256]{1,0:T(8,128)S(1)} %shard_map.52.old_ref), channel_id=1, source_target_pairs={{0,8},{1,9},{4,12},{5,13},{10,2},{11,3},{14,6},{15,7},{16,24},{17,... | collective-permute-start | bytes 786440 | tf_op jit(solution)/shard_map/ppermute | solution.py:219
  68.5 24.6 %collective-permute-start.14 = (f32[256,256]{1,0:T(8,128)S(1)}, f32[256,256]{1,0:T(8,128)S(1)}, u32[]{:S(2)}, u32[]{:S(2)}) collective-permute-start(f32[256,256]{1,0:T(8,128)S(1)} %collective-permute-done.9), channel_id=1, source_target_pairs={{0,0},{1,1},{2,8},{3,9},{4,16},{5,17},{6,24},{7,25},{8,2},{9,3},{1... | collective-permute-start | bytes 786440 | tf_op jit(solution)/shard_map/ppermute | solution.py:219
  72.5 8.0 %collective-permute-start.20 = (f32[128,256]{1,0:T(8,128)S(1)}, f32[128,256]{1,0:T(8,128)S(1)}, u32[]{:S(2)}, u32[]{:S(2)}) collective-permute-start(f32[128,256]{1,0:T(8,128)S(1)} %get-tuple-element.35), channel_id=1, source_target_pairs={{0,16},{1,17},{2,18},{3,19},{4,20},{5,21},{6,22},{7,23},{8,24},{9,... | collective-permute-start | bytes 393224 | tf_op jit(solution)/shard_map/ppermute | solution.py:219
  80.5 12.6 %copy-start.3 = (f32[512,256]{1,0:T(8,128)S(1)}, f32[512,256]{1,0:T(8,128)}, u32[]{:S(2)}) copy-start(f32[512,256]{1,0:T(8,128)} %refs_1_.3) | copy-start | bytes 1572868
  80.5 14.4 %collective-permute-start.21 = (f32[64,256]{1,0:T(8,128)S(1)}, f32[64,256]{1,0:T(8,128)S(1)}, u32[]{:S(2)}, u32[]{:S(2)}) collective-permute-start(f32[64,256]{1,0:T(8,128)S(1)} %get-tuple-element.36), channel_id=1, source_target_pairs={{0,0},{1,1},{2,8},{3,9},{4,16},{5,17},{6,24},{7,25},{8,4},{9,5},{1... | collective-permute-start | bytes 196616 | tf_op jit(solution)/shard_map/ppermute | solution.py:219
  82.6 12.9 %collective-permute-start.22 = (f32[64,256]{1,0:T(8,128)S(1)}, f32[64,256]{1,0:T(8,128)S(1)}, u32[]{:S(2)}, u32[]{:S(2)}) collective-permute-start(f32[64,256]{1,0:T(8,128)S(1)} %get-tuple-element.37), channel_id=1, source_target_pairs={{0,1},{1,0},{2,9},{3,8},{4,17},{5,16},{6,25},{7,24},{8,5},{9,4},{1... | collective-permute-start | bytes 196616 | tf_op jit(solution)/shard_map/ppermute | solution.py:219

commit v2 on v0

--- a/solution.py
+++ b/solution.py
@@ -231,10 +231,12 @@
     parts, turns, col_factors = cut[:row_count], cut[row_count:-1], cut[-1]
     parts = [send(parts[s], lambda i, j, k: (i, j ^ s, k)) if s else parts[s] for s in every]
 
+    turns = [send(turns[d], lambda i, j, k: (i, j, k ^ d)) if d else turns[d] for d in both]
+
     def mirror(d, *deps):
-        return send(after(turns[d], *deps), lambda i, j, k: (j, i, k ^ d))
-
-    mirrored = {fold - 1: mirror(fold - 1, *parts)}
+        return send(after(turns[d], *deps), lambda i, j, k: (j, i, k))
+
+    mirrored = {0: mirror(0)}
 
     shares = call(
         functools.partial(residual_kernel, row_count, fold),
@@ -249,7 +251,6 @@
         got = send(shares[d], lambda i, j, k: (i, j, k ^ d))
         share = call(add_kernel, [shape(piece, width)], [share, got])[0]
 
-    col_factors = after(col_factors, blocks[bits[-1]])
     for bit in reversed(bits):
         got = send(
             col_factors, lambda i, j, k: (i ^ bit, j, k) if (i ^ j) & (2 * bit - 1) == 0 else None
@@ -263,7 +264,7 @@
         for d in both:
             one = chunks[s]
             spread.append(send(one, lambda i, j, k: (i, j, k ^ d)) if d else one)
-    for d in range(fold - 1):
+    for d in range(1, fold):
         mirrored[d] = mirror(d, *chunks)
 
     halves = [pltpu.VMEM((own_rows, width), BF16)] * 2

time: 90.4 us -> 94.5 us (1.045)
  starting transfers between devices: 28 us -> 30.9 us
  waiting for transfers between devices: 55 us -> 56.1 us
    ppermute x22 -> x23, starting transfers between devices: 28 us -> 30.9 us  [send(): return lax.ppermute(value, AXES, pairs)]
    ppermute x22 -> x23, waiting for transfers between devices: 55 us -> 56.1 us  [send(): return lax.ppermute(value, AXES, pairs)]
  transfers between devices with their start and end apart: 22 -> 23, of which waited for: 12 -> 12; matrix products, arithmetic and copies ran while one was open for 0% -> 0% of each run, Pallas kernels for 4% -> 4%
where the time goes in v2:
time: 94.5 us; the launch traced here: 94.2 us
  waiting for transfers between devices  56.1 us (59%)
  starting transfers between devices  30.9 us (33%)
  Pallas kernels  5.13 us (5%)
  local copies, waits for them, and re-layouts  1.25 us (1%)
    ppermute x23, waiting for transfers between devices, send(): return lax.ppermute(value, AXES, pairs)  56.1 us
    ppermute x23, starting transfers between devices, send(): return lax.ppermute(value, AXES, pairs)  30.9 us
    pallas_call x10, Pallas kernels, call(): pl.pallas_call(kernel, out_shape=outs, in_specs=[pl.BlockSpec(memory_spac...  5.13 us
  transfers between devices with their start and end apart: 23, of which 12 were waited for; matrix products, arithmetic and copies ran while one was open for 0% of the time, Pallas kernels for 4%

profile of v2, /device:TPU:4, one launch (start us, length us, event | category | flops | bytes accessed | tf_op | source)
XLA Modules:
  0.0 94.2 jit_solution(13708769278771201548)
XLA Ops:
  0.7 1.2 %copy-done = f32[512,512]{1,0:T(8,128)S(1)} copy-done((f32[512,512]{1,0:T(8,128)S(1)}, f32[512,512]{1,0:T(8,128)}, u32[]{:S(2)}) %copy-start) | copy-done | bytes 1048600
  2.1 13.6 %collective-permute-done.3.refs_6_.refs_5_ = f32[256,512]{1,0:T(8,128)S(1)} collective-permute-done((f32[256,512]{1,0:T(8,128)S(1)}, f32[256,512]{1,0:T(8,128)S(1)}, u32[]{:S(2)}, u32[]{:S(2)}) %collective-permute-start.3) | collective-permute-done | bytes 524320 | tf_op jit(solution)/shard_map/ppermute | solution.py:218
  15.6 0.8 shard_map.50
  16.5 1.6 %collective-permute-start.7 = (f32[128,256]{1,0:T(8,128)S(1)}, f32[128,256]{1,0:T(8,128)S(1)}, u32[]{:S(2)}, u32[]{:S(2)}) collective-permute-start(f32[128,256]{1,0:T(8,128)S(1)} %get-tuple-element.22), channel_id=1, source_target_pairs={{0,2},{1,3},{2,0},{3,1},{4,6},{5,7},{6,4},{7,5},{8,10},{9,11},{10,... | collective-permute-start | bytes 393224 | tf_op jit(solution)/shard_map/ppermute | solution.py:218
  18.1 2.6 %collective-permute-start.8 = (f32[128,256]{1,0:T(8,128)S(1)}, f32[128,256]{1,0:T(8,128)S(1)}, u32[]{:S(2)}, u32[]{:S(2)}) collective-permute-start(f32[128,256]{1,0:T(8,128)S(1)} %get-tuple-element.23), channel_id=1, source_target_pairs={{0,4},{1,5},{2,6},{3,7},{4,0},{5,1},{6,2},{7,3},{8,12},{9,13},{10,... | collective-permute-start | bytes 393224 | tf_op jit(solution)/shard_map/ppermute | solution.py:218
  20.9 3.7 %collective-permute-done.7.refs_1_ = f32[128,256]{1,0:T(8,128)S(1)} collective-permute-done((f32[128,256]{1,0:T(8,128)S(1)}, f32[128,256]{1,0:T(8,128)S(1)}, u32[]{:S(2)}, u32[]{:S(2)}) %collective-permute-start.7) | collective-permute-done | bytes 131104 | tf_op jit(solution)/shard_map/ppermute | solution.py:218
  24.7 6.4 %collective-permute-done.8.refs_2_ = f32[128,256]{1,0:T(8,128)S(1)} collective-permute-done((f32[128,256]{1,0:T(8,128)S(1)}, f32[128,256]{1,0:T(8,128)S(1)}, u32[]{:S(2)}, u32[]{:S(2)}) %collective-permute-start.8) | collective-permute-done | bytes 131104 | tf_op jit(solution)/shard_map/ppermute | solution.py:218
  31.1 0.7 shard_map.53
  31.8 1.6 %collective-permute-start.10 = (f32[64,512]{1,0:T(8,128)S(1)}, f32[64,512]{1,0:T(8,128)S(1)}, u32[]{:S(2)}, u32[]{:S(2)}) collective-permute-start(f32[64,512]{1,0:T(8,128)S(1)} %get-tuple-element.26), channel_id=1, source_target_pairs={{0,1},{1,0},{2,3},{3,2},{4,5},{5,4},{6,7},{7,6},{8,9},{9,8},{10,11... | collective-permute-start | bytes 393224 | tf_op jit(solution)/shard_map/ppermute | solution.py:218
  33.4 3.5 %collective-permute-done.10.right = f32[64,512]{1,0:T(8,128)S(1)} collective-permute-done((f32[64,512]{1,0:T(8,128)S(1)}, f32[64,512]{1,0:T(8,128)S(1)}, u32[]{:S(2)}, u32[]{:S(2)}) %collective-permute-start.10) | collective-permute-done | bytes 131104 | tf_op jit(solution)/shard_map/ppermute | solution.py:218
  36.9 2.5 %collective-permute-start.13 = (f32[64,512]{1,0:T(8,128)S(1)}, f32[64,512]{1,0:T(8,128)S(1)}, u32[]{:S(2)}, u32[]{:S(2)}) collective-permute-start(f32[64,512]{1,0:T(8,128)S(1)} %shard_map.54.refs_9_.refs_0_), channel_id=1, source_target_pairs={{0,6},{1,7},{2,4},{3,5},{4,2},{5,3},{6,0},{7,1},{8,14},{9,15},{10,... | collective-permute-start | bytes 393224 | tf_op jit(solution)/shard_map/ppermute | solution.py:218
  39.4 1.6 %collective-permute-start.12 = (f32[64,512]{1,0:T(8,128)S(1)}, f32[64,512]{1,0:T(8,128)S(1)}, u32[]{:S(2)}, u32[]{:S(2)}) collective-permute-start(f32[64,512]{1,0:T(8,128)S(1)} %shard_map.54.refs_9_.refs_0_), channel_id=1, source_target_pairs={{0,4},{1,5},{2,6},{3,7},{4,0},{5,1},{6,2},{7,3},{8,12},{9,13},{10,... | collective-permute-start | bytes 393224 | tf_op jit(solution)/shard_map/ppermute | solution.py:218
  41.3 1.5 %collective-permute-start.15 = (f32[64,512]{1,0:T(8,128)S(1)}, f32[64,512]{1,0:T(8,128)S(1)}, u32[]{:S(2)}, u32[]{:S(2)}) collective-permute-start(f32[64,512]{1,0:T(8,128)S(1)} %shard_map.54.refs_9_.refs_0_), channel_id=1, source_target_pairs={{0,1},{1,0},{2,3},{3,2},{4,5},{5,4},{6,7},{7,6},{8,9},{9,8},{10,11... | collective-permute-start | bytes 393224 | tf_op jit(solution)/shard_map/ppermute | solution.py:218
  42.8 2.3 %collective-permute-done.13.refs_15_.refs_6_ = f32[64,512]{1,0:T(8,128)S(1)} collective-permute-done((f32[64,512]{1,0:T(8,128)S(1)}, f32[64,512]{1,0:T(8,128)S(1)}, u32[]{:S(2)}, u32[]{:S(2)}) %collective-permute-start.13) | collective-permute-done | bytes 131104 | tf_op jit(solution)/shard_map/ppermute | solution.py:218
  45.1 1.5 %collective-permute-start.18 = (f32[64,512]{1,0:T(8,128)S(1)}, f32[64,512]{1,0:T(8,128)S(1)}, u32[]{:S(2)}, u32[]{:S(2)}) collective-permute-start(f32[64,512]{1,0:T(8,128)S(1)} %collective-permute-done.13.refs_15_.refs_6_), channel_id=1, source_target_pairs={{0,1},{1,0},{2,3},{3,2},{4,5},{5,4},{6,7},{7,6},{8,9},{9,8},{10,11... | collective-permute-start | bytes 393224 | tf_op jit(solution)/shard_map/ppermute | solution.py:218
  46.6 3.4 %collective-permute-done.12.refs_13_.refs_4_ = f32[64,512]{1,0:T(8,128)S(1)} collective-permute-done((f32[64,512]{1,0:T(8,128)S(1)}, f32[64,512]{1,0:T(8,128)S(1)}, u32[]{:S(2)}, u32[]{:S(2)}) %collective-permute-start.12) | collective-permute-done | bytes 131104 | tf_op jit(solution)/shard_map/ppermute | solution.py:218
  50.1 1.5 %collective-permute-start.17 = (f32[64,512]{1,0:T(8,128)S(1)}, f32[64,512]{1,0:T(8,128)S(1)}, u32[]{:S(2)}, u32[]{:S(2)}) collective-permute-start(f32[64,512]{1,0:T(8,128)S(1)} %collective-permute-done.12.refs_13_.refs_4_), channel_id=1, source_target_pairs={{0,1},{1,0},{2,3},{3,2},{4,5},{5,4},{6,7},{7,6},{8,9},{9,8},{10,11... | collective-permute-start | bytes 393224 | tf_op jit(solution)/shard_map/ppermute | solution.py:218
  52.1 1.3 %collective-permute-start = (f32[256,256]{1,0:T(8,128)S(1)}, f32[256,256]{1,0:T(8,128)S(1)}, u32[]{:S(2)}, u32[]{:S(2)}) collective-permute-start(f32[256,256]{1,0:T(8,128)S(1)} %get-tuple-element.18.old_ref), channel_id=1, source_target_pairs={{0,16},{1,17},{10,26},{11,27},{20,4},{21,5},{30,14},{31,15}} | collective-permute-start | bytes 786440 | tf_op jit(solution)/shard_map/ppermute | solution.py:218
  53.4 1.6 %collective-permute-start.6 = (f32[256,256]{1,0:T(8,128)S(1)}, f32[256,256]{1,0:T(8,128)S(1)}, u32[]{:S(2)}, u32[]{:S(2)}) collective-permute-start(f32[256,256]{1,0:T(8,128)S(1)} %get-tuple-element.20), channel_id=1, source_target_pairs={{0,1},{1,0},{2,3},{3,2},{4,5},{5,4},{6,7},{7,6},{8,9},{9,8},{10,11... | collective-permute-start | bytes 786440 | tf_op jit(solution)/shard_map/ppermute | solution.py:218
  55.0 1.5 %collective-permute-done.17.refs_14_.refs_5_ = f32[64,512]{1,0:T(8,128)S(1)} collective-permute-done((f32[64,512]{1,0:T(8,128)S(1)}, f32[64,512]{1,0:T(8,128)S(1)}, u32[]{:S(2)}, u32[]{:S(2)}) %collective-permute-start.17) | collective-permute-done | bytes 131104 | tf_op jit(solution)/shard_map/ppermute | solution.py:218
  56.4 2.7 %collective-permute-done.16.refs_12_.refs_3_ = f32[64,512]{1,0:T(8,128)S(1)} collective-permute-done((f32[64,512]{1,0:T(8,128)S(1)}, f32[64,512]{1,0:T(8,128)S(1)}, u32[]{:S(2)}, u32[]{:S(2)}) %collective-permute-start.16) | collective-permute-done | bytes 131104 | tf_op jit(solution)/shard_map/ppermute | solution.py:218
  59.1 0.9 shard_map.56
  60.1 3.0 %collective-permute-start.5 = (f32[256,256]{1,0:T(8,128)S(1)}, f32[256,256]{1,0:T(8,128)S(1)}, u32[]{:S(2)}, u32[]{:S(2)}) collective-permute-start(f32[256,256]{1,0:T(8,128)S(1)} %get-tuple-element.19), channel_id=1, source_target_pairs={{0,0},{1,1},{2,8},{3,9},{4,16},{5,17},{6,24},{7,25},{8,2},{9,3},{1... | collective-permute-start | bytes 786440 | tf_op jit(solution)/shard_map/ppermute | solution.py:218
  63.1 3.4 %collective-permute-start.1 = (f32[256,256]{1,0:T(8,128)S(1)}, f32[256,256]{1,0:T(8,128)S(1)}, u32[]{:S(2)}, u32[]{:S(2)}) collective-permute-start(f32[256,256]{1,0:T(8,128)S(1)} %shard_map.51.old_ref), channel_id=1, source_target_pairs={{0,8},{1,9},{4,12},{5,13},{10,2},{11,3},{14,6},{15,7},{16,24},{17,... | collective-permute-start | bytes 786440 | tf_op jit(solution)/shard_map/ppermute | solution.py:218
  66.6 3.9 %collective-permute-start.14 = (f32[256,256]{1,0:T(8,128)S(1)}, f32[256,256]{1,0:T(8,128)S(1)}, u32[]{:S(2)}, u32[]{:S(2)}) collective-permute-start(f32[256,256]{1,0:T(8,128)S(1)} %collective-permute-done.6), channel_id=1, source_target_pairs={{0,0},{1,1},{2,8},{3,9},{4,16},{5,17},{6,24},{7,25},{8,2},{9,3},{1... | collective-permute-start | bytes 786440 | tf_op jit(solution)/shard_map/ppermute | solution.py:218
  70.6 7.9 %collective-permute-done.20.got_ref = f32[128,256]{1,0:T(8,128)S(1)} collective-permute-done((f32[128,256]{1,0:T(8,128)S(1)}, f32[128,256]{1,0:T(8,128)S(1)}, u32[]{:S(2)}, u32[]{:S(2)}) %collective-permute-start.20) | collective-permute-done | bytes 131104 | tf_op jit(solution)/shard_map/ppermute | solution.py:218
  78.6 1.9 %collective-permute-start.21 = (f32[64,256]{1,0:T(8,128)S(1)}, f32[64,256]{1,0:T(8,128)S(1)}, u32[]{:S(2)}, u32[]{:S(2)}) collective-permute-start(f32[64,256]{1,0:T(8,128)S(1)} %get-tuple-element.32), channel_id=1, source_target_pairs={{0,0},{1,1},{2,8},{3,9},{4,16},{5,17},{6,24},{7,25},{8,4},{9,5},{1... | collective-permute-start | bytes 196616 | tf_op jit(solution)/shard_map/ppermute | solution.py:218
  80.6 3.5 %collective-permute-done.5.refs_7_ = f32[256,256]{1,0:T(8,128)S(1)} collective-permute-done((f32[256,256]{1,0:T(8,128)S(1)}, f32[256,256]{1,0:T(8,128)S(1)}, u32[]{:S(2)}, u32[]{:S(2)}) %collective-permute-start.5) | collective-permute-done | bytes 262176 | tf_op jit(solution)/shard_map/ppermute | solution.py:218
  84.1 7.0 %collective-permute-done.14.refs_8_ = f32[256,256]{1,0:T(8,128)S(1)} collective-permute-done((f32[256,256]{1,0:T(8,128)S(1)}, f32[256,256]{1,0:T(8,128)S(1)}, u32[]{:S(2)}, u32[]{:S(2)}) %collective-permute-start.14) | collective-permute-done | bytes 262176 | tf_op jit(solution)/shard_map/ppermute | solution.py:218
  91.1 1.9 %shard_map.55 = f32[512,256]{1,0:T(8,128)} custom-call(f32[512,256]{1,0:T(8,128)S(1)} %copy-done.1, f32[512,256]{1,0:T(8,128)S(1)} %copy-done.2, f32[256,256]{1,0:T(8,128)S(1)} %shard_map.52.refs_2_, f32[256,512]{1,0:T(8,128)S(1)} %constant_dynamic-slice_fusion.refs_4_.refs_3_, f32[256,512]{1,0:T(8,128)S(1)} %collective-permute-done.2.refs_5_.refs_4_, ...), custom_call_target="tpu_custom_call" | custom-call | flops 603979776 | bytes 5505024 | tf_op jit(solution)/shard_map/pallas_call | solution.py:50
  93.0 0.5 collective-permute-done.22.refs_1_
  93.6 0.7 shard_map.59
  (31 shorter events, 1.7 us)
Async XLA Ops:
  0.6 1.2 %copy-start = (f32[512,512]{1,0:T(8,128)S(1)}, f32[512,512]{1,0:T(8,128)}, u32[]{:S(2)}) copy-start(f32[512,512]{1,0:T(8,128)} %param.4) | copy-start | bytes 3145732
  1.9 13.8 %copy-start.1 = (f32[512,256]{1,0:T(8,128)S(1)}, f32[512,256]{1,0:T(8,128)}, u32[]{:S(2)}) copy-start(f32[512,256]{1,0:T(8,128)} %refs_8_.1) | copy-start | bytes 1572868
  1.9 13.8 %copy-start.2 = (f32[512,256]{1,0:T(8,128)S(1)}, f32[512,256]{1,0:T(8,128)}, u32[]{:S(2)}) copy-start(f32[512,256]{1,0:T(8,128)} %refs_1_.3) | copy-start | bytes 1572868
  1.9 13.7 %collective-permute-start.3 = (f32[256,512]{1,0:T(8,128)S(1)}, f32[256,512]{1,0:T(8,128)S(1)}, u32[]{:S(2)}, u32[]{:S(2)}) collective-permute-start(f32[256,512]{1,0:T(8,128)S(1)} %constant_dynamic-slice_fusion.refs_4_.refs_3_), channel_id=1, source_target_pairs={{0,16},{1,17},{2,18},{3,19},{4,20},{5,21},{6,22},{7,23},{8,24},{9,... | collective-permute-start | bytes 1572872 | tf_op jit(solution)/shard_map/ppermute | solution.py:218
  2.0 29.1 %collective-permute-start.2 = (f32[256,512]{1,0:T(8,128)S(1)}, f32[256,512]{1,0:T(8,128)S(1)}, u32[]{:S(2)}, u32[]{:S(2)}) collective-permute-start(f32[256,512]{1,0:T(8,128)S(1)} %constant_dynamic-slice_fusion.refs_4_.refs_3_), channel_id=1, source_target_pairs={{0,8},{1,9},{2,10},{3,11},{4,12},{5,13},{6,14},{7,15},{8,0},{9,1},... | collective-permute-start | bytes 1572872 | tf_op jit(solution)/shard_map/ppermute | solution.py:218
  15.6 15.4 %collective-permute-start.4 = (f32[256,512]{1,0:T(8,128)S(1)}, f32[256,512]{1,0:T(8,128)S(1)}, u32[]{:S(2)}, u32[]{:S(2)}) collective-permute-start(f32[256,512]{1,0:T(8,128)S(1)} %collective-permute-done.3.refs_6_.refs_5_), channel_id=1, source_target_pairs={{0,8},{1,9},{2,10},{3,11},{4,12},{5,13},{6,14},{7,15},{8,0},{9,1},... | collective-permute-start | bytes 1572872 | tf_op jit(solution)/shard_map/ppermute | solution.py:218
  16.5 8.2 %collective-permute-start.7 = (f32[128,256]{1,0:T(8,128)S(1)}, f32[128,256]{1,0:T(8,128)S(1)}, u32[]{:S(2)}, u32[]{:S(2)}) collective-permute-start(f32[128,256]{1,0:T(8,128)S(1)} %get-tuple-element.22), channel_id=1, source_target_pairs={{0,2},{1,3},{2,0},{3,1},{4,6},{5,7},{6,4},{7,5},{8,10},{9,11},{10,... | collective-permute-start | bytes 393224 | tf_op jit(solution)/shard_map/ppermute | solution.py:218
  18.1 12.9 %collective-permute-start.8 = (f32[128,256]{1,0:T(8,128)S(1)}, f32[128,256]{1,0:T(8,128)S(1)}, u32[]{:S(2)}, u32[]{:S(2)}) collective-permute-start(f32[128,256]{1,0:T(8,128)S(1)} %get-tuple-element.23), channel_id=1, source_target_pairs={{0,4},{1,5},{2,6},{3,7},{4,0},{5,1},{6,2},{7,3},{8,12},{9,13},{10,... | collective-permute-start | bytes 393224 | tf_op jit(solution)/shard_map/ppermute | solution.py:218
  20.7 10.3 %collective-permute-start.9 = (f32[128,256]{1,0:T(8,128)S(1)}, f32[128,256]{1,0:T(8,128)S(1)}, u32[]{:S(2)}, u32[]{:S(2)}) collective-permute-start(f32[128,256]{1,0:T(8,128)S(1)} %get-tuple-element.24), channel_id=1, source_target_pairs={{0,6},{1,7},{2,4},{3,5},{4,2},{5,3},{6,0},{7,1},{8,14},{9,15},{10,... | collective-permute-start | bytes 393224 | tf_op jit(solution)/shard_map/ppermute | solution.py:218
  31.8 5.0 %collective-permute-start.10 = (f32[64,512]{1,0:T(8,128)S(1)}, f32[64,512]{1,0:T(8,128)S(1)}, u32[]{:S(2)}, u32[]{:S(2)}) collective-permute-start(f32[64,512]{1,0:T(8,128)S(1)} %get-tuple-element.26), channel_id=1, source_target_pairs={{0,1},{1,0},{2,3},{3,2},{4,5},{5,4},{6,7},{7,6},{8,9},{9,8},{10,11... | collective-permute-start | bytes 393224 | tf_op jit(solution)/shard_map/ppermute | solution.py:218
  36.9 8.3 %collective-permute-start.13 = (f32[64,512]{1,0:T(8,128)S(1)}, f32[64,512]{1,0:T(8,128)S(1)}, u32[]{:S(2)}, u32[]{:S(2)}) collective-permute-start(f32[64,512]{1,0:T(8,128)S(1)} %shard_map.54.refs_9_.refs_0_), channel_id=1, source_target_pairs={{0,6},{1,7},{2,4},{3,5},{4,2},{5,3},{6,0},{7,1},{8,14},{9,15},{10,... | collective-permute-start | bytes 393224 | tf_op jit(solution)/shard_map/ppermute | solution.py:218
  39.4 10.7 %collective-permute-start.12 = (f32[64,512]{1,0:T(8,128)S(1)}, f32[64,512]{1,0:T(8,128)S(1)}, u32[]{:S(2)}, u32[]{:S(2)}) collective-permute-start(f32[64,512]{1,0:T(8,128)S(1)} %shard_map.54.refs_9_.refs_0_), channel_id=1, source_target_pairs={{0,4},{1,5},{2,6},{3,7},{4,0},{5,1},{6,2},{7,3},{8,12},{9,13},{10,... | collective-permute-start | bytes 393224 | tf_op jit(solution)/shard_map/ppermute | solution.py:218
  41.0 10.6 %collective-permute-start.11 = (f32[64,512]{1,0:T(8,128)S(1)}, f32[64,512]{1,0:T(8,128)S(1)}, u32[]{:S(2)}, u32[]{:S(2)}) collective-permute-start(f32[64,512]{1,0:T(8,128)S(1)} %shard_map.54.refs_9_.refs_0_), channel_id=1, source_target_pairs={{0,2},{1,3},{2,0},{3,1},{4,6},{5,7},{6,4},{7,5},{8,10},{9,11},{10,... | collective-permute-start | bytes 393224 | tf_op jit(solution)/shard_map/ppermute | solution.py:218
  41.3 12.1 %collective-permute-start.15 = (f32[64,512]{1,0:T(8,128)S(1)}, f32[64,512]{1,0:T(8,128)S(1)}, u32[]{:S(2)}, u32[]{:S(2)}) collective-permute-start(f32[64,512]{1,0:T(8,128)S(1)} %shard_map.54.refs_9_.refs_0_), channel_id=1, source_target_pairs={{0,1},{1,0},{2,3},{3,2},{4,5},{5,4},{6,7},{7,6},{8,9},{9,8},{10,11... | collective-permute-start | bytes 393224 | tf_op jit(solution)/shard_map/ppermute | solution.py:218
  45.1 9.8 %collective-permute-start.18 = (f32[64,512]{1,0:T(8,128)S(1)}, f32[64,512]{1,0:T(8,128)S(1)}, u32[]{:S(2)}, u32[]{:S(2)}) collective-permute-start(f32[64,512]{1,0:T(8,128)S(1)} %collective-permute-done.13.refs_15_.refs_6_), channel_id=1, source_target_pairs={{0,1},{1,0},{2,3},{3,2},{4,5},{5,4},{6,7},{7,6},{8,9},{9,8},{10,11... | collective-permute-start | bytes 393224 | tf_op jit(solution)/shard_map/ppermute | solution.py:218
  50.1 6.4 %collective-permute-start.17 = (f32[64,512]{1,0:T(8,128)S(1)}, f32[64,512]{1,0:T(8,128)S(1)}, u32[]{:S(2)}, u32[]{:S(2)}) collective-permute-start(f32[64,512]{1,0:T(8,128)S(1)} %collective-permute-done.12.refs_13_.refs_4_), channel_id=1, source_target_pairs={{0,1},{1,0},{2,3},{3,2},{4,5},{5,4},{6,7},{7,6},{8,9},{9,8},{10,11... | collective-permute-start | bytes 393224 | tf_op jit(solution)/shard_map/ppermute | solution.py:218
  51.6 7.5 %collective-permute-start.16 = (f32[64,512]{1,0:T(8,128)S(1)}, f32[64,512]{1,0:T(8,128)S(1)}, u32[]{:S(2)}, u32[]{:S(2)}) collective-permute-start(f32[64,512]{1,0:T(8,128)S(1)} %collective-permute-done.11.refs_11_.refs_2_), channel_id=1, source_target_pairs={{0,1},{1,0},{2,3},{3,2},{4,5},{5,4},{6,7},{7,6},{8,9},{9,8},{10,11... | collective-permute-start | bytes 393224 | tf_op jit(solution)/shard_map/ppermute | solution.py:218
  52.1 11.0 %collective-permute-start = (f32[256,256]{1,0:T(8,128)S(1)}, f32[256,256]{1,0:T(8,128)S(1)}, u32[]{:S(2)}, u32[]{:S(2)}) collective-permute-start(f32[256,256]{1,0:T(8,128)S(1)} %get-tuple-element.18.old_ref), channel_id=1, source_target_pairs={{0,16},{1,17},{10,26},{11,27},{20,4},{21,5},{30,14},{31,15}} | collective-permute-start | bytes 786440 | tf_op jit(solution)/shard_map/ppermute | solution.py:218
  53.4 13.2 %collective-permute-start.6 = (f32[256,256]{1,0:T(8,128)S(1)}, f32[256,256]{1,0:T(8,128)S(1)}, u32[]{:S(2)}, u32[]{:S(2)}) collective-permute-start(f32[256,256]{1,0:T(8,128)S(1)} %get-tuple-element.20), channel_id=1, source_target_pairs={{0,1},{1,0},{2,3},{3,2},{4,5},{5,4},{6,7},{7,6},{8,9},{9,8},{10,11... | collective-permute-start | bytes 786440 | tf_op jit(solution)/shard_map/ppermute | solution.py:218
  60.0 10.5 %collective-permute-start.19 = (f32[256,256]{1,0:T(8,128)S(1)}, f32[256,256]{1,0:T(8,128)S(1)}, u32[]{:S(2)}, u32[]{:S(2)}) collective-permute-start(f32[256,256]{1,0:T(8,128)S(1)} %get-tuple-element.29), channel_id=1, source_target_pairs={{0,8},{1,9},{2,10},{3,11},{4,12},{5,13},{6,14},{7,15},{8,0},{9,1},... | collective-permute-start | bytes 786440 | tf_op jit(solution)/shard_map/ppermute | solution.py:218
  60.1 24.0 %collective-permute-start.5 = (f32[256,256]{1,0:T(8,128)S(1)}, f32[256,256]{1,0:T(8,128)S(1)}, u32[]{:S(2)}, u32[]{:S(2)}) collective-permute-start(f32[256,256]{1,0:T(8,128)S(1)} %get-tuple-element.19), channel_id=1, source_target_pairs={{0,0},{1,1},{2,8},{3,9},{4,16},{5,17},{6,24},{7,25},{8,2},{9,3},{1... | collective-permute-start | bytes 786440 | tf_op jit(solution)/shard_map/ppermute | solution.py:218
  63.1 17.5 %collective-permute-start.1 = (f32[256,256]{1,0:T(8,128)S(1)}, f32[256,256]{1,0:T(8,128)S(1)}, u32[]{:S(2)}, u32[]{:S(2)}) collective-permute-start(f32[256,256]{1,0:T(8,128)S(1)} %shard_map.51.old_ref), channel_id=1, source_target_pairs={{0,8},{1,9},{4,12},{5,13},{10,2},{11,3},{14,6},{15,7},{16,24},{17,... | collective-permute-start | bytes 786440 | tf_op jit(solution)/shard_map/ppermute | solution.py:218
  66.6 24.6 %collective-permute-start.14 = (f32[256,256]{1,0:T(8,128)S(1)}, f32[256,256]{1,0:T(8,128)S(1)}, u32[]{:S(2)}, u32[]{:S(2)}) collective-permute-start(f32[256,256]{1,0:T(8,128)S(1)} %collective-permute-done.6), channel_id=1, source_target_pairs={{0,0},{1,1},{2,8},{3,9},{4,16},{5,17},{6,24},{7,25},{8,2},{9,3},{1... | collective-permute-start | bytes 786440 | tf_op jit(solution)/shard_map/ppermute | solution.py:218
  70.5 8.0 %collective-permute-start.20 = (f32[128,256]{1,0:T(8,128)S(1)}, f32[128,256]{1,0:T(8,128)S(1)}, u32[]{:S(2)}, u32[]{:S(2)}) collective-permute-start(f32[128,256]{1,0:T(8,128)S(1)} %get-tuple-element.31), channel_id=1, source_target_pairs={{0,16},{1,17},{2,18},{3,19},{4,20},{5,21},{6,22},{7,23},{8,24},{9,... | collective-permute-start | bytes 393224 | tf_op jit(solution)/shard_map/ppermute | solution.py:218
  78.6 14.4 %collective-permute-start.21 = (f32[64,256]{1,0:T(8,128)S(1)}, f32[64,256]{1,0:T(8,128)S(1)}, u32[]{:S(2)}, u32[]{:S(2)}) collective-permute-start(f32[64,256]{1,0:T(8,128)S(1)} %get-tuple-element.32), channel_id=1, source_target_pairs={{0,0},{1,1},{2,8},{3,9},{4,16},{5,17},{6,24},{7,25},{8,4},{9,5},{1... | collective-permute-start | bytes 196616 | tf_op jit(solution)/shard_map/ppermute | solution.py:218
  80.5 13.0 %collective-permute-start.22 = (f32[64,256]{1,0:T(8,128)S(1)}, f32[64,256]{1,0:T(8,128)S(1)}, u32[]{:S(2)}, u32[]{:S(2)}) collective-permute-start(f32[64,256]{1,0:T(8,128)S(1)} %get-tuple-element.33), channel_id=1, source_target_pairs={{0,1},{1,0},{2,9},{3,8},{4,17},{5,16},{6,25},{7,24},{8,5},{9,4},{1... | collective-permute-start | bytes 196616 | tf_op jit(solution)/shard_map/ppermute | solution.py:218

commit v3 on v2

--- a/solution.py
+++ b/solution.py
@@ -258,7 +258,11 @@
         picked = functools.partial(pick_kernel, bit, fold)
         col_factors = call(picked, [shape(*got.shape)], [col_factors, got])[0]
 
-    chunks = [send(share, lambda i, j, k: (i, j ^ s, k)) if s else share for s in every]
+    chunks = {0: share}
+    for bit in reversed(bits):
+        for s in list(chunks):
+            chunks[s | bit] = send(chunks[s], lambda i, j, k: (i, j ^ bit, k))
+    chunks = [chunks[s] for s in every]
     spread = []
     for s in every:
         for d in both:

time: 94.5 us -> 94.6 us (level)
  waiting for transfers between devices: 56.1 us -> 57.9 us
  starting transfers between devices: 30.9 us -> 29.3 us
    ppermute x23, waiting for transfers between devices: 56.1 us -> 57.9 us  [send(): return lax.ppermute(value, AXES, pairs)]
    ppermute x23, starting transfers between devices: 30.9 us -> 29.3 us  [send(): return lax.ppermute(value, AXES, pairs)]
  transfers between devices with their start and end apart: 23 -> 23, of which waited for: 12 -> 13; matrix products, arithmetic and copies ran while one was open for 0% -> 0% of each run, Pallas kernels for 4% -> 4%
where the time goes in v3:
time: 94.6 us; the launch traced here: 94.4 us
  waiting for transfers between devices  57.9 us (61%)
  starting transfers between devices  29.3 us (31%)
  Pallas kernels  5.14 us (5%)
  local copies, waits for them, and re-layouts  1.25 us (1%)
    ppermute x23, waiting for transfers between devices, send(): return lax.ppermute(value, AXES, pairs)  57.9 us
    ppermute x23, starting transfers between devices, send(): return lax.ppermute(value, AXES, pairs)  29.3 us
    pallas_call x10, Pallas kernels, call(): pl.pallas_call(kernel, out_shape=outs, in_specs=[pl.BlockSpec(memory_spac...  5.14 us
  transfers between devices with their start and end apart: 23, of which 13 were waited for; matrix products, arithmetic and copies ran while one was open for 0% of the time, Pallas kernels for 4%

profile of v3, /device:TPU:4, one launch (start us, length us, event | category | flops | bytes accessed | tf_op | source)
XLA Modules:
  0.0 94.4 jit_solution(12492226883432401947)
XLA Ops:
  0.7 1.2 %copy-done = f32[512,512]{1,0:T(8,128)S(1)} copy-done((f32[512,512]{1,0:T(8,128)S(1)}, f32[512,512]{1,0:T(8,128)}, u32[]{:S(2)}) %copy-start) | copy-done | bytes 1048600
  2.1 13.6 %collective-permute-done.3.refs_6_.refs_5_ = f32[256,512]{1,0:T(8,128)S(1)} collective-permute-done((f32[256,512]{1,0:T(8,128)S(1)}, f32[256,512]{1,0:T(8,128)S(1)}, u32[]{:S(2)}, u32[]{:S(2)}) %collective-permute-start.3) | collective-permute-done | bytes 524320 | tf_op jit(solution)/shard_map/ppermute | solution.py:218
  15.6 0.8 shard_map.50
  16.5 1.6 %collective-permute-start.7 = (f32[128,256]{1,0:T(8,128)S(1)}, f32[128,256]{1,0:T(8,128)S(1)}, u32[]{:S(2)}, u32[]{:S(2)}) collective-permute-start(f32[128,256]{1,0:T(8,128)S(1)} %get-tuple-element.22), channel_id=1, source_target_pairs={{0,2},{1,3},{2,0},{3,1},{4,6},{5,7},{6,4},{7,5},{8,10},{9,11},{10,... | collective-permute-start | bytes 393224 | tf_op jit(solution)/shard_map/ppermute | solution.py:218
  18.1 2.6 %collective-permute-start.8 = (f32[128,256]{1,0:T(8,128)S(1)}, f32[128,256]{1,0:T(8,128)S(1)}, u32[]{:S(2)}, u32[]{:S(2)}) collective-permute-start(f32[128,256]{1,0:T(8,128)S(1)} %get-tuple-element.23), channel_id=1, source_target_pairs={{0,4},{1,5},{2,6},{3,7},{4,0},{5,1},{6,2},{7,3},{8,12},{9,13},{10,... | collective-permute-start | bytes 393224 | tf_op jit(solution)/shard_map/ppermute | solution.py:218
  20.9 3.7 %collective-permute-done.7.refs_1_ = f32[128,256]{1,0:T(8,128)S(1)} collective-permute-done((f32[128,256]{1,0:T(8,128)S(1)}, f32[128,256]{1,0:T(8,128)S(1)}, u32[]{:S(2)}, u32[]{:S(2)}) %collective-permute-start.7) | collective-permute-done | bytes 131104 | tf_op jit(solution)/shard_map/ppermute | solution.py:218
  24.7 6.4 %collective-permute-done.8.refs_2_ = f32[128,256]{1,0:T(8,128)S(1)} collective-permute-done((f32[128,256]{1,0:T(8,128)S(1)}, f32[128,256]{1,0:T(8,128)S(1)}, u32[]{:S(2)}, u32[]{:S(2)}) %collective-permute-start.8) | collective-permute-done | bytes 131104 | tf_op jit(solution)/shard_map/ppermute | solution.py:218
  31.1 0.7 shard_map.53
  31.8 1.6 %collective-permute-start.10 = (f32[64,512]{1,0:T(8,128)S(1)}, f32[64,512]{1,0:T(8,128)S(1)}, u32[]{:S(2)}, u32[]{:S(2)}) collective-permute-start(f32[64,512]{1,0:T(8,128)S(1)} %get-tuple-element.26), channel_id=1, source_target_pairs={{0,1},{1,0},{2,3},{3,2},{4,5},{5,4},{6,7},{7,6},{8,9},{9,8},{10,11... | collective-permute-start | bytes 393224 | tf_op jit(solution)/shard_map/ppermute | solution.py:218
  33.4 3.5 %collective-permute-done.10.right = f32[64,512]{1,0:T(8,128)S(1)} collective-permute-done((f32[64,512]{1,0:T(8,128)S(1)}, f32[64,512]{1,0:T(8,128)S(1)}, u32[]{:S(2)}, u32[]{:S(2)}) %collective-permute-start.10) | collective-permute-done | bytes 131104 | tf_op jit(solution)/shard_map/ppermute | solution.py:218
  36.9 3.7 %collective-permute-start.12 = (f32[64,512]{1,0:T(8,128)S(1)}, f32[64,512]{1,0:T(8,128)S(1)}, u32[]{:S(2)}, u32[]{:S(2)}) collective-permute-start(f32[64,512]{1,0:T(8,128)S(1)} %shard_map.54.refs_9_.refs_0_), channel_id=1, source_target_pairs={{0,4},{1,5},{2,6},{3,7},{4,0},{5,1},{6,2},{7,3},{8,12},{9,13},{10,... | collective-permute-start | bytes 393224 | tf_op jit(solution)/shard_map/ppermute | solution.py:218
  40.5 4.8 %collective-permute-done.12.refs_13_.refs_4_ = f32[64,512]{1,0:T(8,128)S(1)} collective-permute-done((f32[64,512]{1,0:T(8,128)S(1)}, f32[64,512]{1,0:T(8,128)S(1)}, u32[]{:S(2)}, u32[]{:S(2)}) %collective-permute-start.12) | collective-permute-done | bytes 131104 | tf_op jit(solution)/shard_map/ppermute | solution.py:218
  45.5 1.5 %collective-permute-start.15 = (f32[64,512]{1,0:T(8,128)S(1)}, f32[64,512]{1,0:T(8,128)S(1)}, u32[]{:S(2)}, u32[]{:S(2)}) collective-permute-start(f32[64,512]{1,0:T(8,128)S(1)} %shard_map.54.refs_9_.refs_0_), channel_id=1, source_target_pairs={{0,1},{1,0},{2,3},{3,2},{4,5},{5,4},{6,7},{7,6},{8,9},{9,8},{10,11... | collective-permute-start | bytes 393224 | tf_op jit(solution)/shard_map/ppermute | solution.py:218
  47.6 1.5 %collective-permute-start.16 = (f32[64,512]{1,0:T(8,128)S(1)}, f32[64,512]{1,0:T(8,128)S(1)}, u32[]{:S(2)}, u32[]{:S(2)}) collective-permute-start(f32[64,512]{1,0:T(8,128)S(1)} %collective-permute-done.11.refs_11_.refs_2_), channel_id=1, source_target_pairs={{0,1},{1,0},{2,3},{3,2},{4,5},{5,4},{6,7},{7,6},{8,9},{9,8},{10,11... | collective-permute-start | bytes 393224 | tf_op jit(solution)/shard_map/ppermute | solution.py:218
  49.1 1.2 %collective-permute-done.13.refs_15_.refs_6_ = f32[64,512]{1,0:T(8,128)S(1)} collective-permute-done((f32[64,512]{1,0:T(8,128)S(1)}, f32[64,512]{1,0:T(8,128)S(1)}, u32[]{:S(2)}, u32[]{:S(2)}) %collective-permute-start.13) | collective-permute-done | bytes 131104 | tf_op jit(solution)/shard_map/ppermute | solution.py:218
  50.3 1.5 %collective-permute-start.18 = (f32[64,512]{1,0:T(8,128)S(1)}, f32[64,512]{1,0:T(8,128)S(1)}, u32[]{:S(2)}, u32[]{:S(2)}) collective-permute-start(f32[64,512]{1,0:T(8,128)S(1)} %collective-permute-done.13.refs_15_.refs_6_), channel_id=1, source_target_pairs={{0,1},{1,0},{2,3},{3,2},{4,5},{5,4},{6,7},{7,6},{8,9},{9,8},{10,11... | collective-permute-start | bytes 393224 | tf_op jit(solution)/shard_map/ppermute | solution.py:218
  51.8 1.3 %collective-permute-start = (f32[256,256]{1,0:T(8,128)S(1)}, f32[256,256]{1,0:T(8,128)S(1)}, u32[]{:S(2)}, u32[]{:S(2)}) collective-permute-start(f32[256,256]{1,0:T(8,128)S(1)} %get-tuple-element.18.old_ref), channel_id=1, source_target_pairs={{0,16},{1,17},{10,26},{11,27},{20,4},{21,5},{30,14},{31,15}} | collective-permute-start | bytes 786440 | tf_op jit(solution)/shard_map/ppermute | solution.py:218
  53.1 0.6 collective-permute-start.6
  53.7 1.0 %collective-permute-done.17.refs_14_.refs_5_ = f32[64,512]{1,0:T(8,128)S(1)} collective-permute-done((f32[64,512]{1,0:T(8,128)S(1)}, f32[64,512]{1,0:T(8,128)S(1)}, u32[]{:S(2)}, u32[]{:S(2)}) %collective-permute-start.17) | collective-permute-done | bytes 131104 | tf_op jit(solution)/shard_map/ppermute | solution.py:218
  54.7 2.8 %collective-permute-done.16.refs_12_.refs_3_ = f32[64,512]{1,0:T(8,128)S(1)} collective-permute-done((f32[64,512]{1,0:T(8,128)S(1)}, f32[64,512]{1,0:T(8,128)S(1)}, u32[]{:S(2)}, u32[]{:S(2)}) %collective-permute-start.16) | collective-permute-done | bytes 131104 | tf_op jit(solution)/shard_map/ppermute | solution.py:218
  57.5 1.8 %collective-permute-done.18.refs_16_.refs_7_ = f32[64,512]{1,0:T(8,128)S(1)} collective-permute-done((f32[64,512]{1,0:T(8,128)S(1)}, f32[64,512]{1,0:T(8,128)S(1)}, u32[]{:S(2)}, u32[]{:S(2)}) %collective-permute-start.18) | collective-permute-done | bytes 131104 | tf_op jit(solution)/shard_map/ppermute | solution.py:218
  59.4 0.9 shard_map.56
  60.4 2.6 %collective-permute-start.5 = (f32[256,256]{1,0:T(8,128)S(1)}, f32[256,256]{1,0:T(8,128)S(1)}, u32[]{:S(2)}, u32[]{:S(2)}) collective-permute-start(f32[256,256]{1,0:T(8,128)S(1)} %get-tuple-element.19), channel_id=1, source_target_pairs={{0,0},{1,1},{2,8},{3,9},{4,16},{5,17},{6,24},{7,25},{8,2},{9,3},{1... | collective-permute-start | bytes 786440 | tf_op jit(solution)/shard_map/ppermute | solution.py:218
  63.0 3.2 %collective-permute-start.1 = (f32[256,256]{1,0:T(8,128)S(1)}, f32[256,256]{1,0:T(8,128)S(1)}, u32[]{:S(2)}, u32[]{:S(2)}) collective-permute-start(f32[256,256]{1,0:T(8,128)S(1)} %shard_map.51.old_ref), channel_id=1, source_target_pairs={{0,8},{1,9},{4,12},{5,13},{10,2},{11,3},{14,6},{15,7},{16,24},{17,... | collective-permute-start | bytes 786440 | tf_op jit(solution)/shard_map/ppermute | solution.py:218
  66.3 4.1 %collective-permute-start.14 = (f32[256,256]{1,0:T(8,128)S(1)}, f32[256,256]{1,0:T(8,128)S(1)}, u32[]{:S(2)}, u32[]{:S(2)}) collective-permute-start(f32[256,256]{1,0:T(8,128)S(1)} %collective-permute-done.6), channel_id=1, source_target_pairs={{0,0},{1,1},{2,8},{3,9},{4,16},{5,17},{6,24},{7,25},{8,2},{9,3},{1... | collective-permute-start | bytes 786440 | tf_op jit(solution)/shard_map/ppermute | solution.py:218
  70.5 8.3 %collective-permute-done.20.got_ref = f32[128,256]{1,0:T(8,128)S(1)} collective-permute-done((f32[128,256]{1,0:T(8,128)S(1)}, f32[128,256]{1,0:T(8,128)S(1)}, u32[]{:S(2)}, u32[]{:S(2)}) %collective-permute-start.20) | collective-permute-done | bytes 131104 | tf_op jit(solution)/shard_map/ppermute | solution.py:218
  78.8 1.9 %collective-permute-start.21 = (f32[64,256]{1,0:T(8,128)S(1)}, f32[64,256]{1,0:T(8,128)S(1)}, u32[]{:S(2)}, u32[]{:S(2)}) collective-permute-start(f32[64,256]{1,0:T(8,128)S(1)} %get-tuple-element.32), channel_id=1, source_target_pairs={{0,0},{1,1},{2,8},{3,9},{4,16},{5,17},{6,24},{7,25},{8,4},{9,5},{1... | collective-permute-start | bytes 196616 | tf_op jit(solution)/shard_map/ppermute | solution.py:218
  81.1 3.3 %collective-permute-done.5.refs_7_ = f32[256,256]{1,0:T(8,128)S(1)} collective-permute-done((f32[256,256]{1,0:T(8,128)S(1)}, f32[256,256]{1,0:T(8,128)S(1)}, u32[]{:S(2)}, u32[]{:S(2)}) %collective-permute-start.5) | collective-permute-done | bytes 262176 | tf_op jit(solution)/shard_map/ppermute | solution.py:218
  84.5 6.7 %collective-permute-done.14.refs_8_ = f32[256,256]{1,0:T(8,128)S(1)} collective-permute-done((f32[256,256]{1,0:T(8,128)S(1)}, f32[256,256]{1,0:T(8,128)S(1)}, u32[]{:S(2)}, u32[]{:S(2)}) %collective-permute-start.14) | collective-permute-done | bytes 262176 | tf_op jit(solution)/shard_map/ppermute | solution.py:218
  91.2 1.9 %shard_map.55 = f32[512,256]{1,0:T(8,128)} custom-call(f32[512,256]{1,0:T(8,128)S(1)} %copy-done.1, f32[512,256]{1,0:T(8,128)S(1)} %copy-done.2, f32[256,256]{1,0:T(8,128)S(1)} %shard_map.52.refs_2_, f32[256,512]{1,0:T(8,128)S(1)} %constant_dynamic-slice_fusion.refs_4_.refs_3_, f32[256,512]{1,0:T(8,128)S(1)} %collective-permute-done.2.refs_5_.refs_4_, ...), custom_call_target="tpu_custom_call" | custom-call | flops 603979776 | bytes 5505024 | tf_op jit(solution)/shard_map/pallas_call | solution.py:50
  93.0 0.7 collective-permute-done.22.refs_1_
  93.7 0.7 shard_map.59
  (31 shorter events, 1.8 us)
Async XLA Ops:
  0.6 1.2 %copy-start = (f32[512,512]{1,0:T(8,128)S(1)}, f32[512,512]{1,0:T(8,128)}, u32[]{:S(2)}) copy-start(f32[512,512]{1,0:T(8,128)} %param.4) | copy-start | bytes 3145732
  1.9 13.8 %copy-start.1 = (f32[512,256]{1,0:T(8,128)S(1)}, f32[512,256]{1,0:T(8,128)}, u32[]{:S(2)}) copy-start(f32[512,256]{1,0:T(8,128)} %refs_8_.1) | copy-start | bytes 1572868
  1.9 13.8 %copy-start.2 = (f32[512,256]{1,0:T(8,128)S(1)}, f32[512,256]{1,0:T(8,128)}, u32[]{:S(2)}) copy-start(f32[512,256]{1,0:T(8,128)} %refs_1_.3) | copy-start | bytes 1572868
  1.9 13.7 %collective-permute-start.3 = (f32[256,512]{1,0:T(8,128)S(1)}, f32[256,512]{1,0:T(8,128)S(1)}, u32[]{:S(2)}, u32[]{:S(2)}) collective-permute-start(f32[256,512]{1,0:T(8,128)S(1)} %constant_dynamic-slice_fusion.refs_4_.refs_3_), channel_id=1, source_target_pairs={{0,16},{1,17},{2,18},{3,19},{4,20},{5,21},{6,22},{7,23},{8,24},{9,... | collective-permute-start | bytes 1572872 | tf_op jit(solution)/shard_map/ppermute | solution.py:218
  2.0 29.1 %collective-permute-start.2 = (f32[256,512]{1,0:T(8,128)S(1)}, f32[256,512]{1,0:T(8,128)S(1)}, u32[]{:S(2)}, u32[]{:S(2)}) collective-permute-start(f32[256,512]{1,0:T(8,128)S(1)} %constant_dynamic-slice_fusion.refs_4_.refs_3_), channel_id=1, source_target_pairs={{0,8},{1,9},{2,10},{3,11},{4,12},{5,13},{6,14},{7,15},{8,0},{9,1},... | collective-permute-start | bytes 1572872 | tf_op jit(solution)/shard_map/ppermute | solution.py:218
  15.6 15.4 %collective-permute-start.4 = (f32[256,512]{1,0:T(8,128)S(1)}, f32[256,512]{1,0:T(8,128)S(1)}, u32[]{:S(2)}, u32[]{:S(2)}) collective-permute-start(f32[256,512]{1,0:T(8,128)S(1)} %collective-permute-done.3.refs_6_.refs_5_), channel_id=1, source_target_pairs={{0,8},{1,9},{2,10},{3,11},{4,12},{5,13},{6,14},{7,15},{8,0},{9,1},... | collective-permute-start | bytes 1572872 | tf_op jit(solution)/shard_map/ppermute | solution.py:218
  16.5 8.2 %collective-permute-start.7 = (f32[128,256]{1,0:T(8,128)S(1)}, f32[128,256]{1,0:T(8,128)S(1)}, u32[]{:S(2)}, u32[]{:S(2)}) collective-permute-start(f32[128,256]{1,0:T(8,128)S(1)} %get-tuple-element.22), channel_id=1, source_target_pairs={{0,2},{1,3},{2,0},{3,1},{4,6},{5,7},{6,4},{7,5},{8,10},{9,11},{10,... | collective-permute-start | bytes 393224 | tf_op jit(solution)/shard_map/ppermute | solution.py:218
  18.1 12.9 %collective-permute-start.8 = (f32[128,256]{1,0:T(8,128)S(1)}, f32[128,256]{1,0:T(8,128)S(1)}, u32[]{:S(2)}, u32[]{:S(2)}) collective-permute-start(f32[128,256]{1,0:T(8,128)S(1)} %get-tuple-element.23), channel_id=1, source_target_pairs={{0,4},{1,5},{2,6},{3,7},{4,0},{5,1},{6,2},{7,3},{8,12},{9,13},{10,... | collective-permute-start | bytes 393224 | tf_op jit(solution)/shard_map/ppermute | solution.py:218
  20.7 10.3 %collective-permute-start.9 = (f32[128,256]{1,0:T(8,128)S(1)}, f32[128,256]{1,0:T(8,128)S(1)}, u32[]{:S(2)}, u32[]{:S(2)}) collective-permute-start(f32[128,256]{1,0:T(8,128)S(1)} %get-tuple-element.24), channel_id=1, source_target_pairs={{0,6},{1,7},{2,4},{3,5},{4,2},{5,3},{6,0},{7,1},{8,14},{9,15},{10,... | collective-permute-start | bytes 393224 | tf_op jit(solution)/shard_map/ppermute | solution.py:218
  31.8 5.0 %collective-permute-start.10 = (f32[64,512]{1,0:T(8,128)S(1)}, f32[64,512]{1,0:T(8,128)S(1)}, u32[]{:S(2)}, u32[]{:S(2)}) collective-permute-start(f32[64,512]{1,0:T(8,128)S(1)} %get-tuple-element.26), channel_id=1, source_target_pairs={{0,1},{1,0},{2,3},{3,2},{4,5},{5,4},{6,7},{7,6},{8,9},{9,8},{10,11... | collective-permute-start | bytes 393224 | tf_op jit(solution)/shard_map/ppermute | solution.py:218
  36.9 8.5 %collective-permute-start.12 = (f32[64,512]{1,0:T(8,128)S(1)}, f32[64,512]{1,0:T(8,128)S(1)}, u32[]{:S(2)}, u32[]{:S(2)}) collective-permute-start(f32[64,512]{1,0:T(8,128)S(1)} %shard_map.54.refs_9_.refs_0_), channel_id=1, source_target_pairs={{0,4},{1,5},{2,6},{3,7},{4,0},{5,1},{6,2},{7,3},{8,12},{9,13},{10,... | collective-permute-start | bytes 393224 | tf_op jit(solution)/shard_map/ppermute | solution.py:218
  40.5 7.1 %collective-permute-start.11 = (f32[64,512]{1,0:T(8,128)S(1)}, f32[64,512]{1,0:T(8,128)S(1)}, u32[]{:S(2)}, u32[]{:S(2)}) collective-permute-start(f32[64,512]{1,0:T(8,128)S(1)} %shard_map.54.refs_9_.refs_0_), channel_id=1, source_target_pairs={{0,2},{1,3},{2,0},{3,1},{4,6},{5,7},{6,4},{7,5},{8,10},{9,11},{10,... | collective-permute-start | bytes 393224 | tf_op jit(solution)/shard_map/ppermute | solution.py:218
  45.3 5.0 %collective-permute-start.13 = (f32[64,512]{1,0:T(8,128)S(1)}, f32[64,512]{1,0:T(8,128)S(1)}, u32[]{:S(2)}, u32[]{:S(2)}) collective-permute-start(f32[64,512]{1,0:T(8,128)S(1)} %collective-permute-done.12.refs_13_.refs_4_), channel_id=1, source_target_pairs={{0,2},{1,3},{2,0},{3,1},{4,6},{5,7},{6,4},{7,5},{8,10},{9,11},{10,... | collective-permute-start | bytes 393224 | tf_op jit(solution)/shard_map/ppermute | solution.py:218
  45.5 7.5 %collective-permute-start.15 = (f32[64,512]{1,0:T(8,128)S(1)}, f32[64,512]{1,0:T(8,128)S(1)}, u32[]{:S(2)}, u32[]{:S(2)}) collective-permute-start(f32[64,512]{1,0:T(8,128)S(1)} %shard_map.54.refs_9_.refs_0_), channel_id=1, source_target_pairs={{0,1},{1,0},{2,3},{3,2},{4,5},{5,4},{6,7},{7,6},{8,9},{9,8},{10,11... | collective-permute-start | bytes 393224 | tf_op jit(solution)/shard_map/ppermute | solution.py:218
  47.0 7.7 %collective-permute-start.17 = (f32[64,512]{1,0:T(8,128)S(1)}, f32[64,512]{1,0:T(8,128)S(1)}, u32[]{:S(2)}, u32[]{:S(2)}) collective-permute-start(f32[64,512]{1,0:T(8,128)S(1)} %collective-permute-done.12.refs_13_.refs_4_), channel_id=1, source_target_pairs={{0,1},{1,0},{2,3},{3,2},{4,5},{5,4},{6,7},{7,6},{8,9},{9,8},{10,11... | collective-permute-start | bytes 393224 | tf_op jit(solution)/shard_map/ppermute | solution.py:218
  47.6 10.0 %collective-permute-start.16 = (f32[64,512]{1,0:T(8,128)S(1)}, f32[64,512]{1,0:T(8,128)S(1)}, u32[]{:S(2)}, u32[]{:S(2)}) collective-permute-start(f32[64,512]{1,0:T(8,128)S(1)} %collective-permute-done.11.refs_11_.refs_2_), channel_id=1, source_target_pairs={{0,1},{1,0},{2,3},{3,2},{4,5},{5,4},{6,7},{7,6},{8,9},{9,8},{10,11... | collective-permute-start | bytes 393224 | tf_op jit(solution)/shard_map/ppermute | solution.py:218
  50.3 9.1 %collective-permute-start.18 = (f32[64,512]{1,0:T(8,128)S(1)}, f32[64,512]{1,0:T(8,128)S(1)}, u32[]{:S(2)}, u32[]{:S(2)}) collective-permute-start(f32[64,512]{1,0:T(8,128)S(1)} %collective-permute-done.13.refs_15_.refs_6_), channel_id=1, source_target_pairs={{0,1},{1,0},{2,3},{3,2},{4,5},{5,4},{6,7},{7,6},{8,9},{9,8},{10,11... | collective-permute-start | bytes 393224 | tf_op jit(solution)/shard_map/ppermute | solution.py:218
  51.8 11.2 %collective-permute-start = (f32[256,256]{1,0:T(8,128)S(1)}, f32[256,256]{1,0:T(8,128)S(1)}, u32[]{:S(2)}, u32[]{:S(2)}) collective-permute-start(f32[256,256]{1,0:T(8,128)S(1)} %get-tuple-element.18.old_ref), channel_id=1, source_target_pairs={{0,16},{1,17},{10,26},{11,27},{20,4},{21,5},{30,14},{31,15}} | collective-permute-start | bytes 786440 | tf_op jit(solution)/shard_map/ppermute | solution.py:218
  53.1 13.2 %collective-permute-start.6 = (f32[256,256]{1,0:T(8,128)S(1)}, f32[256,256]{1,0:T(8,128)S(1)}, u32[]{:S(2)}, u32[]{:S(2)}) collective-permute-start(f32[256,256]{1,0:T(8,128)S(1)} %get-tuple-element.20), channel_id=1, source_target_pairs={{0,1},{1,0},{2,3},{3,2},{4,5},{5,4},{6,7},{7,6},{8,9},{9,8},{10,11... | collective-permute-start | bytes 786440 | tf_op jit(solution)/shard_map/ppermute | solution.py:218
  60.3 10.1 %collective-permute-start.19 = (f32[256,256]{1,0:T(8,128)S(1)}, f32[256,256]{1,0:T(8,128)S(1)}, u32[]{:S(2)}, u32[]{:S(2)}) collective-permute-start(f32[256,256]{1,0:T(8,128)S(1)} %get-tuple-element.29), channel_id=1, source_target_pairs={{0,8},{1,9},{2,10},{3,11},{4,12},{5,13},{6,14},{7,15},{8,0},{9,1},... | collective-permute-start | bytes 786440 | tf_op jit(solution)/shard_map/ppermute | solution.py:218
  60.4 24.1 %collective-permute-start.5 = (f32[256,256]{1,0:T(8,128)S(1)}, f32[256,256]{1,0:T(8,128)S(1)}, u32[]{:S(2)}, u32[]{:S(2)}) collective-permute-start(f32[256,256]{1,0:T(8,128)S(1)} %get-tuple-element.19), channel_id=1, source_target_pairs={{0,0},{1,1},{2,8},{3,9},{4,16},{5,17},{6,24},{7,25},{8,2},{9,3},{1... | collective-permute-start | bytes 786440 | tf_op jit(solution)/shard_map/ppermute | solution.py:218
  63.0 18.1 %collective-permute-start.1 = (f32[256,256]{1,0:T(8,128)S(1)}, f32[256,256]{1,0:T(8,128)S(1)}, u32[]{:S(2)}, u32[]{:S(2)}) collective-permute-start(f32[256,256]{1,0:T(8,128)S(1)} %shard_map.51.old_ref), channel_id=1, source_target_pairs={{0,8},{1,9},{4,12},{5,13},{10,2},{11,3},{14,6},{15,7},{16,24},{17,... | collective-permute-start | bytes 786440 | tf_op jit(solution)/shard_map/ppermute | solution.py:218
  66.3 24.9 %collective-permute-start.14 = (f32[256,256]{1,0:T(8,128)S(1)}, f32[256,256]{1,0:T(8,128)S(1)}, u32[]{:S(2)}, u32[]{:S(2)}) collective-permute-start(f32[256,256]{1,0:T(8,128)S(1)} %collective-permute-done.6), channel_id=1, source_target_pairs={{0,0},{1,1},{2,8},{3,9},{4,16},{5,17},{6,24},{7,25},{8,2},{9,3},{1... | collective-permute-start | bytes 786440 | tf_op jit(solution)/shard_map/ppermute | solution.py:218
  70.5 8.4 %collective-permute-start.20 = (f32[128,256]{1,0:T(8,128)S(1)}, f32[128,256]{1,0:T(8,128)S(1)}, u32[]{:S(2)}, u32[]{:S(2)}) collective-permute-start(f32[128,256]{1,0:T(8,128)S(1)} %get-tuple-element.31), channel_id=1, source_target_pairs={{0,16},{1,17},{2,18},{3,19},{4,20},{5,21},{6,22},{7,23},{8,24},{9,... | collective-permute-start | bytes 393224 | tf_op jit(solution)/shard_map/ppermute | solution.py:218
  78.8 14.2 %collective-permute-start.21 = (f32[64,256]{1,0:T(8,128)S(1)}, f32[64,256]{1,0:T(8,128)S(1)}, u32[]{:S(2)}, u32[]{:S(2)}) collective-permute-start(f32[64,256]{1,0:T(8,128)S(1)} %get-tuple-element.32), channel_id=1, source_target_pairs={{0,0},{1,1},{2,8},{3,9},{4,16},{5,17},{6,24},{7,25},{8,4},{9,5},{1... | collective-permute-start | bytes 196616 | tf_op jit(solution)/shard_map/ppermute | solution.py:218
  80.8 13.0 %collective-permute-start.22 = (f32[64,256]{1,0:T(8,128)S(1)}, f32[64,256]{1,0:T(8,128)S(1)}, u32[]{:S(2)}, u32[]{:S(2)}) collective-permute-start(f32[64,256]{1,0:T(8,128)S(1)} %get-tuple-element.33), channel_id=1, source_target_pairs={{0,1},{1,0},{2,9},{3,8},{4,17},{5,16},{6,25},{7,24},{8,5},{9,4},{1... | collective-permute-start | bytes 196616 | tf_op jit(solution)/shard_map/ppermute | solution.py:218

commit v4 on v3

--- a/solution.py
+++ b/solution.py
@@ -9,10 +9,6 @@
 
 AXES = ("row", "col")
 F32, BF16 = jnp.float32, jnp.bfloat16
-
-
-def after(value, *others):
-    return lax.optimization_barrier((value, *others))[0]
 
 
 def split(value):
@@ -172,8 +168,8 @@
 
 def coeff_kernel(count, fold, *refs):
     coeffs, factors, col_factors = refs[:3]
-    blocks, mirrored = refs[3 : 3 + count], refs[3 + count : 3 + count + fold]
-    chunks, (out, high, low) = refs[3 + count + fold : -3], refs[-3:]
+    blocks, mirrored = refs[3 : 3 + count], refs[3 + count : 4 + count + fold]
+    chunks, (out, high, low) = refs[4 + count + fold : -3], refs[-3:]
     r, q, b = place(fold)
     assemble(chunks, high, low, fold, q, b)
     features = blocks[0][...]
@@ -184,9 +180,10 @@
     rows = mirrored[0].shape[0]
     for e in range(fold):
         at = slice(e * rows, (e + 1) * rows)
-        turned = mirrored[0][...]
+        crossed = ((r ^ q) & (count // 2)) != 0
+        turned = jnp.where(crossed, mirrored[1][...], mirrored[0][...])
         for d in range(1, fold):
-            turned = jnp.where((b ^ e) == d, mirrored[d][...], turned)
+            turned = jnp.where((b ^ e) == d, mirrored[d + 1][...], turned)
         turned = turned.T
         own = coeffs[at]
         symmetric = 0.5 * (own * own + turned * turned)
@@ -233,10 +230,13 @@
 
     turns = [send(turns[d], lambda i, j, k: (i, j, k ^ d)) if d else turns[d] for d in both]
 
-    def mirror(d, *deps):
-        return send(after(turns[d], *deps), lambda i, j, k: (j, i, k))
-
-    mirrored = {0: mirror(0)}
+    far = row_count // 2
+    hopped = send(turns[0], lambda i, j, k: (i ^ far, j, k) if (i ^ j) & far else None)
+    mirrored = [
+        send(turns[0], lambda i, j, k: None if (i ^ j) & far else (j, i, k)),
+        send(hopped, lambda i, j, k: None if (i ^ j) & far else (j, i ^ far, k)),
+        *(send(turns[d], lambda i, j, k: (j, i, k)) for d in both if d),
+    ]
 
     shares = call(
         functools.partial(residual_kernel, row_count, fold),
@@ -268,8 +268,6 @@
         for d in both:
             one = chunks[s]
             spread.append(send(one, lambda i, j, k: (i, j, k ^ d)) if d else one)
-    for d in range(1, fold):
-        mirrored[d] = mirror(d, *chunks)
 
     halves = [pltpu.VMEM((own_rows, width), BF16)] * 2
     give, keep = call(
@@ -312,7 +310,7 @@
     grad_coeffs = call(
         functools.partial(coeff_kernel, row_count, fold),
         [shape(own_rows, own_cols)],
-        [coeffs, factors, col_factors, *blocks, *[mirrored[d] for d in both], *spread],
+        [coeffs, factors, col_factors, *blocks, *mirrored, *spread],
         scratch=halves,
         flops=6 * own_rows * own_cols * (width + factors.shape[1]),
         grant=12,

time: 94.6 us -> 89.8 us (0.949)
  the two profiles are of different devices: /device:TPU:4 before, /device:TPU:5 now
where the time goes in v4:
time: 89.8 us; the launch traced here: 89.6 us
  starting transfers between devices  43.4 us (48%)
  waiting for transfers between devices  39 us (43%)
  Pallas kernels  5.14 us (6%)
  local copies, waits for them, and re-layouts  1.25 us (1%)
    ppermute x25, starting transfers between devices, send(): return lax.ppermute(value, AXES, pairs)  43.4 us
    ppermute x25, waiting for transfers between devices, send(): return lax.ppermute(value, AXES, pairs)  39 us
    pallas_call x10, Pallas kernels, call(): pl.pallas_call(kernel, out_shape=outs, in_specs=[pl.BlockSpec(memory_spac...  5.14 us
  transfers between devices with their start and end apart: 25, of which 9 were waited for; matrix products, arithmetic and copies ran while one was open for 0% of the time, Pallas kernels for 4%

profile of v4, /device:TPU:5, one launch (start us, length us, event | category | flops | bytes accessed | tf_op | source)
XLA Modules:
  0.0 89.6 jit_solution(13573385422867273398)
XLA Ops:
  0.7 1.2 %copy-done = f32[512,512]{1,0:T(8,128)S(1)} copy-done((f32[512,512]{1,0:T(8,128)S(1)}, f32[512,512]{1,0:T(8,128)}, u32[]{:S(2)}) %copy-start) | copy-done | bytes 1048600
  2.0 0.7 collective-permute-start.2
  2.7 12.1 %collective-permute-done.3.refs_6_.refs_5_ = f32[256,512]{1,0:T(8,128)S(1)} collective-permute-done((f32[256,512]{1,0:T(8,128)S(1)}, f32[256,512]{1,0:T(8,128)S(1)}, u32[]{:S(2)}, u32[]{:S(2)}) %collective-permute-start.3) | collective-permute-done | bytes 524320 | tf_op jit(solution)/shard_map/ppermute | solution.py:215
  14.8 1.5 %collective-permute-start.4 = (f32[256,512]{1,0:T(8,128)S(1)}, f32[256,512]{1,0:T(8,128)S(1)}, u32[]{:S(2)}, u32[]{:S(2)}) collective-permute-start(f32[256,512]{1,0:T(8,128)S(1)} %collective-permute-done.3.refs_6_.refs_5_), channel_id=1, source_target_pairs={{0,8},{1,9},{2,10},{3,11},{4,12},{5,13},{6,14},{7,15},{8,0},{9,1},... | collective-permute-start | bytes 1572872 | tf_op jit(solution)/shard_map/ppermute | solution.py:215
  16.3 0.8 shard_map.50
  17.1 1.4 %collective-permute-start.10 = (f32[128,256]{1,0:T(8,128)S(1)}, f32[128,256]{1,0:T(8,128)S(1)}, u32[]{:S(2)}, u32[]{:S(2)}) collective-permute-start(f32[128,256]{1,0:T(8,128)S(1)} %get-tuple-element.21), channel_id=1, source_target_pairs={{0,2},{1,3},{2,0},{3,1},{4,6},{5,7},{6,4},{7,5},{8,10},{9,11},{10,... | collective-permute-start | bytes 393224 | tf_op jit(solution)/shard_map/ppermute | solution.py:215
  18.5 2.3 %collective-permute-start.11 = (f32[128,256]{1,0:T(8,128)S(1)}, f32[128,256]{1,0:T(8,128)S(1)}, u32[]{:S(2)}, u32[]{:S(2)}) collective-permute-start(f32[128,256]{1,0:T(8,128)S(1)} %get-tuple-element.22), channel_id=1, source_target_pairs={{0,4},{1,5},{2,6},{3,7},{4,0},{5,1},{6,2},{7,3},{8,12},{9,13},{10,... | collective-permute-start | bytes 393224 | tf_op jit(solution)/shard_map/ppermute | solution.py:215
  20.8 3.5 %collective-permute-done.10.refs_1_ = f32[128,256]{1,0:T(8,128)S(1)} collective-permute-done((f32[128,256]{1,0:T(8,128)S(1)}, f32[128,256]{1,0:T(8,128)S(1)}, u32[]{:S(2)}, u32[]{:S(2)}) %collective-permute-start.10) | collective-permute-done | bytes 131104 | tf_op jit(solution)/shard_map/ppermute | solution.py:215
  24.3 5.6 %collective-permute-done.12.refs_3_ = f32[128,256]{1,0:T(8,128)S(1)} collective-permute-done((f32[128,256]{1,0:T(8,128)S(1)}, f32[128,256]{1,0:T(8,128)S(1)}, u32[]{:S(2)}, u32[]{:S(2)}) %collective-permute-start.12) | collective-permute-done | bytes 131104 | tf_op jit(solution)/shard_map/ppermute | solution.py:215
  29.9 0.7 shard_map.53
  30.6 1.3 %collective-permute-start.13 = (f32[64,512]{1,0:T(8,128)S(1)}, f32[64,512]{1,0:T(8,128)S(1)}, u32[]{:S(2)}, u32[]{:S(2)}) collective-permute-start(f32[64,512]{1,0:T(8,128)S(1)} %get-tuple-element.25), channel_id=1, source_target_pairs={{0,1},{1,0},{2,3},{3,2},{4,5},{5,4},{6,7},{7,6},{8,9},{9,8},{10,11... | collective-permute-start | bytes 393224 | tf_op jit(solution)/shard_map/ppermute | solution.py:215
  31.9 2.6 %collective-permute-done.13.right = f32[64,512]{1,0:T(8,128)S(1)} collective-permute-done((f32[64,512]{1,0:T(8,128)S(1)}, f32[64,512]{1,0:T(8,128)S(1)}, u32[]{:S(2)}, u32[]{:S(2)}) %collective-permute-start.13) | collective-permute-done | bytes 131104 | tf_op jit(solution)/shard_map/ppermute | solution.py:215
  34.5 4.1 %collective-permute-start.17 = (f32[64,512]{1,0:T(8,128)S(1)}, f32[64,512]{1,0:T(8,128)S(1)}, u32[]{:S(2)}, u32[]{:S(2)}) collective-permute-start(f32[64,512]{1,0:T(8,128)S(1)} %shard_map.54.refs_10_.refs_0_), channel_id=1, source_target_pairs={{0,4},{1,5},{2,6},{3,7},{4,0},{5,1},{6,2},{7,3},{8,12},{9,13},{10,... | collective-permute-start | bytes 393224 | tf_op jit(solution)/shard_map/ppermute | solution.py:215
  38.6 4.3 %collective-permute-done.17.refs_14_.refs_4_ = f32[64,512]{1,0:T(8,128)S(1)} collective-permute-done((f32[64,512]{1,0:T(8,128)S(1)}, f32[64,512]{1,0:T(8,128)S(1)}, u32[]{:S(2)}, u32[]{:S(2)}) %collective-permute-start.17) | collective-permute-done | bytes 131104 | tf_op jit(solution)/shard_map/ppermute | solution.py:215
  42.9 1.2 %collective-permute-start.14 = (f32[64,512]{1,0:T(8,128)S(1)}, f32[64,512]{1,0:T(8,128)S(1)}, u32[]{:S(2)}, u32[]{:S(2)}) collective-permute-start(f32[64,512]{1,0:T(8,128)S(1)} %shard_map.54.refs_10_.refs_0_), channel_id=1, source_target_pairs={{0,1},{1,0},{2,3},{3,2},{4,5},{5,4},{6,7},{7,6},{8,9},{9,8},{10,11... | collective-permute-start | bytes 393224 | tf_op jit(solution)/shard_map/ppermute | solution.py:215
  44.4 1.2 %collective-permute-start.16 = (f32[64,512]{1,0:T(8,128)S(1)}, f32[64,512]{1,0:T(8,128)S(1)}, u32[]{:S(2)}, u32[]{:S(2)}) collective-permute-start(f32[64,512]{1,0:T(8,128)S(1)} %collective-permute-done.15.refs_12_.refs_2_), channel_id=1, source_target_pairs={{0,1},{1,0},{2,3},{3,2},{4,5},{5,4},{6,7},{7,6},{8,9},{9,8},{10,11... | collective-permute-start | bytes 393224 | tf_op jit(solution)/shard_map/ppermute | solution.py:215
  45.6 1.5 %collective-permute-done.19.refs_16_.refs_6_ = f32[64,512]{1,0:T(8,128)S(1)} collective-permute-done((f32[64,512]{1,0:T(8,128)S(1)}, f32[64,512]{1,0:T(8,128)S(1)}, u32[]{:S(2)}, u32[]{:S(2)}) %collective-permute-start.19) | collective-permute-done | bytes 131104 | tf_op jit(solution)/shard_map/ppermute | solution.py:215
  47.1 1.2 %collective-permute-start.20 = (f32[64,512]{1,0:T(8,128)S(1)}, f32[64,512]{1,0:T(8,128)S(1)}, u32[]{:S(2)}, u32[]{:S(2)}) collective-permute-start(f32[64,512]{1,0:T(8,128)S(1)} %collective-permute-done.19.refs_16_.refs_6_), channel_id=1, source_target_pairs={{0,1},{1,0},{2,3},{3,2},{4,5},{5,4},{6,7},{7,6},{8,9},{9,8},{10,11... | collective-permute-start | bytes 393224 | tf_op jit(solution)/shard_map/ppermute | solution.py:215
  49.3 2.1 %collective-permute-start.6 = (f32[256,256]{1,0:T(8,128)S(1)}, f32[256,256]{1,0:T(8,128)S(1)}, u32[]{:S(2)}, u32[]{:S(2)}) collective-permute-start(f32[256,256]{1,0:T(8,128)S(1)} %get-tuple-element.18), channel_id=1, source_target_pairs={{4,20},{5,21},{6,22},{7,23},{12,28},{13,29},{14,30},{15,31},{16,0}... | collective-permute-start | bytes 786440 | tf_op jit(solution)/shard_map/ppermute | solution.py:215
  51.5 1.6 %collective-permute-done.20.refs_17_.refs_7_ = f32[64,512]{1,0:T(8,128)S(1)} collective-permute-done((f32[64,512]{1,0:T(8,128)S(1)}, f32[64,512]{1,0:T(8,128)S(1)}, u32[]{:S(2)}, u32[]{:S(2)}) %collective-permute-start.20) | collective-permute-done | bytes 131104 | tf_op jit(solution)/shard_map/ppermute | solution.py:215
  53.1 0.9 shard_map.56
  53.9 7.1 %collective-permute-start.21 = (f32[256,256]{1,0:T(8,128)S(1)}, f32[256,256]{1,0:T(8,128)S(1)}, u32[]{:S(2)}, u32[]{:S(2)}) collective-permute-start(f32[256,256]{1,0:T(8,128)S(1)} %get-tuple-element.27), channel_id=1, source_target_pairs={{0,8},{1,9},{2,10},{3,11},{4,12},{5,13},{6,14},{7,15},{8,0},{9,1},... | collective-permute-start | bytes 786440 | tf_op jit(solution)/shard_map/ppermute | solution.py:215
  61.1 1.3 %collective-permute-start.1 = (f32[256,256]{1,0:T(8,128)S(1)}, f32[256,256]{1,0:T(8,128)S(1)}, u32[]{:S(2)}, u32[]{:S(2)}) collective-permute-start(f32[256,256]{1,0:T(8,128)S(1)} %shard_map.51.old_ref), channel_id=1, source_target_pairs={{0,8},{1,9},{4,12},{5,13},{10,2},{11,3},{14,6},{15,7},{16,24},{17,... | collective-permute-start | bytes 786440 | tf_op jit(solution)/shard_map/ppermute | solution.py:215
  62.4 0.7 collective-permute-start.5
  63.1 3.4 %collective-permute-start.9 = (f32[256,256]{1,0:T(8,128)S(1)}, f32[256,256]{1,0:T(8,128)S(1)}, u32[]{:S(2)}, u32[]{:S(2)}) collective-permute-start(f32[256,256]{1,0:T(8,128)S(1)} %collective-permute-done.8), channel_id=1, source_target_pairs={{0,0},{1,1},{2,8},{3,9},{4,16},{5,17},{6,24},{7,25},{8,2},{9,3},{1... | collective-permute-start | bytes 786440 | tf_op jit(solution)/shard_map/ppermute | solution.py:215
  66.5 1.3 %collective-permute-start.7 = (f32[256,256]{1,0:T(8,128)S(1)}, f32[256,256]{1,0:T(8,128)S(1)}, u32[]{:S(2)}, u32[]{:S(2)}) collective-permute-start(f32[256,256]{1,0:T(8,128)S(1)} %collective-permute-done.6), channel_id=1, source_target_pairs={{0,4},{1,5},{2,12},{3,13},{8,6},{9,7},{10,14},{11,15},{20,16},{21,... | collective-permute-start | bytes 786440 | tf_op jit(solution)/shard_map/ppermute | solution.py:215
  67.9 3.9 %collective-permute-start.22 = (f32[128,256]{1,0:T(8,128)S(1)}, f32[128,256]{1,0:T(8,128)S(1)}, u32[]{:S(2)}, u32[]{:S(2)}) collective-permute-start(f32[128,256]{1,0:T(8,128)S(1)} %get-tuple-element.29), channel_id=1, source_target_pairs={{0,16},{1,17},{2,18},{3,19},{4,20},{5,21},{6,22},{7,23},{8,24},{9,... | collective-permute-start | bytes 393224 | tf_op jit(solution)/shard_map/ppermute | solution.py:215
  71.8 5.8 %collective-permute-done.22.got_ref = f32[128,256]{1,0:T(8,128)S(1)} collective-permute-done((f32[128,256]{1,0:T(8,128)S(1)}, f32[128,256]{1,0:T(8,128)S(1)}, u32[]{:S(2)}, u32[]{:S(2)}) %collective-permute-start.22) | collective-permute-done | bytes 131104 | tf_op jit(solution)/shard_map/ppermute | solution.py:215
  77.6 3.9 %collective-permute-start.23 = (f32[64,256]{1,0:T(8,128)S(1)}, f32[64,256]{1,0:T(8,128)S(1)}, u32[]{:S(2)}, u32[]{:S(2)}) collective-permute-start(f32[64,256]{1,0:T(8,128)S(1)} %get-tuple-element.30), channel_id=1, source_target_pairs={{0,0},{1,1},{2,8},{3,9},{4,16},{5,17},{6,24},{7,25},{8,4},{9,5},{1... | collective-permute-start | bytes 196616 | tf_op jit(solution)/shard_map/ppermute | solution.py:215
  81.6 3.4 %collective-permute-start.24 = (f32[64,256]{1,0:T(8,128)S(1)}, f32[64,256]{1,0:T(8,128)S(1)}, u32[]{:S(2)}, u32[]{:S(2)}) collective-permute-start(f32[64,256]{1,0:T(8,128)S(1)} %get-tuple-element.31), channel_id=1, source_target_pairs={{0,1},{1,0},{2,9},{3,8},{4,17},{5,16},{6,25},{7,24},{8,5},{9,4},{1... | collective-permute-start | bytes 196616 | tf_op jit(solution)/shard_map/ppermute | solution.py:215
  85.0 1.9 %shard_map.55 = f32[512,256]{1,0:T(8,128)} custom-call(f32[512,256]{1,0:T(8,128)S(1)} %copy-done.1, f32[512,256]{1,0:T(8,128)S(1)} %copy-done.2, f32[256,256]{1,0:T(8,128)S(1)} %shard_map.52.refs_2_, f32[256,512]{1,0:T(8,128)S(1)} %constant_dynamic-slice_fusion.refs_4_.refs_3_, f32[256,512]{1,0:T(8,128)S(1)} %collective-permute-done.2.refs_5_.refs_4_, ...), custom_call_target="tpu_custom_call" | custom-call | flops 603979776 | bytes 5767168 | tf_op jit(solution)/shard_map/pallas_call | solution.py:46
  86.9 2.0 %collective-permute-done.24.refs_1_ = f32[64,256]{1,0:T(8,128)S(1)} collective-permute-done((f32[64,256]{1,0:T(8,128)S(1)}, f32[64,256]{1,0:T(8,128)S(1)}, u32[]{:S(2)}, u32[]{:S(2)}) %collective-permute-start.24) | collective-permute-done | bytes 65568 | tf_op jit(solution)/shard_map/ppermute | solution.py:215
  (35 shorter events, 2.2 us)
Async XLA Ops:
  0.6 1.2 %copy-start = (f32[512,512]{1,0:T(8,128)S(1)}, f32[512,512]{1,0:T(8,128)}, u32[]{:S(2)}) copy-start(f32[512,512]{1,0:T(8,128)} %param.4) | copy-start | bytes 3145732
  1.9 14.4 %copy-start.1 = (f32[512,256]{1,0:T(8,128)S(1)}, f32[512,256]{1,0:T(8,128)}, u32[]{:S(2)}) copy-start(f32[512,256]{1,0:T(8,128)} %refs_8_.1) | copy-start | bytes 1572868
  1.9 14.4 %copy-start.2 = (f32[512,256]{1,0:T(8,128)S(1)}, f32[512,256]{1,0:T(8,128)}, u32[]{:S(2)}) copy-start(f32[512,256]{1,0:T(8,128)} %refs_1_.3) | copy-start | bytes 1572868
  1.9 12.9 %collective-permute-start.3 = (f32[256,512]{1,0:T(8,128)S(1)}, f32[256,512]{1,0:T(8,128)S(1)}, u32[]{:S(2)}, u32[]{:S(2)}) collective-permute-start(f32[256,512]{1,0:T(8,128)S(1)} %constant_dynamic-slice_fusion.refs_4_.refs_3_), channel_id=1, source_target_pairs={{0,16},{1,17},{2,18},{3,19},{4,20},{5,21},{6,22},{7,23},{8,24},{9,... | collective-permute-start | bytes 1572872 | tf_op jit(solution)/shard_map/ppermute | solution.py:215
  2.0 27.9 %collective-permute-start.2 = (f32[256,512]{1,0:T(8,128)S(1)}, f32[256,512]{1,0:T(8,128)S(1)}, u32[]{:S(2)}, u32[]{:S(2)}) collective-permute-start(f32[256,512]{1,0:T(8,128)S(1)} %constant_dynamic-slice_fusion.refs_4_.refs_3_), channel_id=1, source_target_pairs={{0,8},{1,9},{2,10},{3,11},{4,12},{5,13},{6,14},{7,15},{8,0},{9,1},... | collective-permute-start | bytes 1572872 | tf_op jit(solution)/shard_map/ppermute | solution.py:215
  14.8 15.1 %collective-permute-start.4 = (f32[256,512]{1,0:T(8,128)S(1)}, f32[256,512]{1,0:T(8,128)S(1)}, u32[]{:S(2)}, u32[]{:S(2)}) collective-permute-start(f32[256,512]{1,0:T(8,128)S(1)} %collective-permute-done.3.refs_6_.refs_5_), channel_id=1, source_target_pairs={{0,8},{1,9},{2,10},{3,11},{4,12},{5,13},{6,14},{7,15},{8,0},{9,1},... | collective-permute-start | bytes 1572872 | tf_op jit(solution)/shard_map/ppermute | solution.py:215
  17.1 7.2 %collective-permute-start.10 = (f32[128,256]{1,0:T(8,128)S(1)}, f32[128,256]{1,0:T(8,128)S(1)}, u32[]{:S(2)}, u32[]{:S(2)}) collective-permute-start(f32[128,256]{1,0:T(8,128)S(1)} %get-tuple-element.21), channel_id=1, source_target_pairs={{0,2},{1,3},{2,0},{3,1},{4,6},{5,7},{6,4},{7,5},{8,10},{9,11},{10,... | collective-permute-start | bytes 393224 | tf_op jit(solution)/shard_map/ppermute | solution.py:215
  18.5 5.8 %collective-permute-start.11 = (f32[128,256]{1,0:T(8,128)S(1)}, f32[128,256]{1,0:T(8,128)S(1)}, u32[]{:S(2)}, u32[]{:S(2)}) collective-permute-start(f32[128,256]{1,0:T(8,128)S(1)} %get-tuple-element.22), channel_id=1, source_target_pairs={{0,4},{1,5},{2,6},{3,7},{4,0},{5,1},{6,2},{7,3},{8,12},{9,13},{10,... | collective-permute-start | bytes 393224 | tf_op jit(solution)/shard_map/ppermute | solution.py:215
  20.8 9.1 %collective-permute-start.12 = (f32[128,256]{1,0:T(8,128)S(1)}, f32[128,256]{1,0:T(8,128)S(1)}, u32[]{:S(2)}, u32[]{:S(2)}) collective-permute-start(f32[128,256]{1,0:T(8,128)S(1)} %get-tuple-element.23), channel_id=1, source_target_pairs={{0,6},{1,7},{2,4},{3,5},{4,2},{5,3},{6,0},{7,1},{8,14},{9,15},{10,... | collective-permute-start | bytes 393224 | tf_op jit(solution)/shard_map/ppermute | solution.py:215
  30.6 3.9 %collective-permute-start.13 = (f32[64,512]{1,0:T(8,128)S(1)}, f32[64,512]{1,0:T(8,128)S(1)}, u32[]{:S(2)}, u32[]{:S(2)}) collective-permute-start(f32[64,512]{1,0:T(8,128)S(1)} %get-tuple-element.25), channel_id=1, source_target_pairs={{0,1},{1,0},{2,3},{3,2},{4,5},{5,4},{6,7},{7,6},{8,9},{9,8},{10,11... | collective-permute-start | bytes 393224 | tf_op jit(solution)/shard_map/ppermute | solution.py:215
  34.5 8.4 %collective-permute-start.17 = (f32[64,512]{1,0:T(8,128)S(1)}, f32[64,512]{1,0:T(8,128)S(1)}, u32[]{:S(2)}, u32[]{:S(2)}) collective-permute-start(f32[64,512]{1,0:T(8,128)S(1)} %shard_map.54.refs_10_.refs_0_), channel_id=1, source_target_pairs={{0,4},{1,5},{2,6},{3,7},{4,0},{5,1},{6,2},{7,3},{8,12},{9,13},{10,... | collective-permute-start | bytes 393224 | tf_op jit(solution)/shard_map/ppermute | solution.py:215
  38.6 5.8 %collective-permute-start.15 = (f32[64,512]{1,0:T(8,128)S(1)}, f32[64,512]{1,0:T(8,128)S(1)}, u32[]{:S(2)}, u32[]{:S(2)}) collective-permute-start(f32[64,512]{1,0:T(8,128)S(1)} %shard_map.54.refs_10_.refs_0_), channel_id=1, source_target_pairs={{0,2},{1,3},{2,0},{3,1},{4,6},{5,7},{6,4},{7,5},{8,10},{9,11},{10,... | collective-permute-start | bytes 393224 | tf_op jit(solution)/shard_map/ppermute | solution.py:215
  42.9 4.2 %collective-permute-start.19 = (f32[64,512]{1,0:T(8,128)S(1)}, f32[64,512]{1,0:T(8,128)S(1)}, u32[]{:S(2)}, u32[]{:S(2)}) collective-permute-start(f32[64,512]{1,0:T(8,128)S(1)} %collective-permute-done.17.refs_14_.refs_4_), channel_id=1, source_target_pairs={{0,2},{1,3},{2,0},{3,1},{4,6},{5,7},{6,4},{7,5},{8,10},{9,11},{10,... | collective-permute-start | bytes 393224 | tf_op jit(solution)/shard_map/ppermute | solution.py:215
  42.9 6.1 %collective-permute-start.14 = (f32[64,512]{1,0:T(8,128)S(1)}, f32[64,512]{1,0:T(8,128)S(1)}, u32[]{:S(2)}, u32[]{:S(2)}) collective-permute-start(f32[64,512]{1,0:T(8,128)S(1)} %shard_map.54.refs_10_.refs_0_), channel_id=1, source_target_pairs={{0,1},{1,0},{2,3},{3,2},{4,5},{5,4},{6,7},{7,6},{8,9},{9,8},{10,11... | collective-permute-start | bytes 393224 | tf_op jit(solution)/shard_map/ppermute | solution.py:215
  44.1 5.2 %collective-permute-start.18 = (f32[64,512]{1,0:T(8,128)S(1)}, f32[64,512]{1,0:T(8,128)S(1)}, u32[]{:S(2)}, u32[]{:S(2)}) collective-permute-start(f32[64,512]{1,0:T(8,128)S(1)} %collective-permute-done.17.refs_14_.refs_4_), channel_id=1, source_target_pairs={{0,1},{1,0},{2,3},{3,2},{4,5},{5,4},{6,7},{7,6},{8,9},{9,8},{10,11... | collective-permute-start | bytes 393224 | tf_op jit(solution)/shard_map/ppermute | solution.py:215
  44.4 7.1 %collective-permute-start.16 = (f32[64,512]{1,0:T(8,128)S(1)}, f32[64,512]{1,0:T(8,128)S(1)}, u32[]{:S(2)}, u32[]{:S(2)}) collective-permute-start(f32[64,512]{1,0:T(8,128)S(1)} %collective-permute-done.15.refs_12_.refs_2_), channel_id=1, source_target_pairs={{0,1},{1,0},{2,3},{3,2},{4,5},{5,4},{6,7},{7,6},{8,9},{9,8},{10,11... | collective-permute-start | bytes 393224 | tf_op jit(solution)/shard_map/ppermute | solution.py:215
  47.1 5.9 %collective-permute-start.20 = (f32[64,512]{1,0:T(8,128)S(1)}, f32[64,512]{1,0:T(8,128)S(1)}, u32[]{:S(2)}, u32[]{:S(2)}) collective-permute-start(f32[64,512]{1,0:T(8,128)S(1)} %collective-permute-done.19.refs_16_.refs_6_), channel_id=1, source_target_pairs={{0,1},{1,0},{2,3},{3,2},{4,5},{5,4},{6,7},{7,6},{8,9},{9,8},{10,11... | collective-permute-start | bytes 393224 | tf_op jit(solution)/shard_map/ppermute | solution.py:215
  48.3 12.7 %collective-permute-start = (f32[256,256]{1,0:T(8,128)S(1)}, f32[256,256]{1,0:T(8,128)S(1)}, u32[]{:S(2)}, u32[]{:S(2)}) collective-permute-start(f32[256,256]{1,0:T(8,128)S(1)} %get-tuple-element.17.old_ref), channel_id=1, source_target_pairs={{0,16},{1,17},{10,26},{11,27},{20,4},{21,5},{30,14},{31,15}} | collective-permute-start | bytes 786440 | tf_op jit(solution)/shard_map/ppermute | solution.py:215
  49.0 14.0 %collective-permute-start.8 = (f32[256,256]{1,0:T(8,128)S(1)}, f32[256,256]{1,0:T(8,128)S(1)}, u32[]{:S(2)}, u32[]{:S(2)}) collective-permute-start(f32[256,256]{1,0:T(8,128)S(1)} %get-tuple-element.19), channel_id=1, source_target_pairs={{0,1},{1,0},{2,3},{3,2},{4,5},{5,4},{6,7},{7,6},{8,9},{9,8},{10,11... | collective-permute-start | bytes 786440 | tf_op jit(solution)/shard_map/ppermute | solution.py:215
  49.3 17.1 %collective-permute-start.6 = (f32[256,256]{1,0:T(8,128)S(1)}, f32[256,256]{1,0:T(8,128)S(1)}, u32[]{:S(2)}, u32[]{:S(2)}) collective-permute-start(f32[256,256]{1,0:T(8,128)S(1)} %get-tuple-element.18), channel_id=1, source_target_pairs={{4,20},{5,21},{6,22},{7,23},{12,28},{13,29},{14,30},{15,31},{16,0}... | collective-permute-start | bytes 786440 | tf_op jit(solution)/shard_map/ppermute | solution.py:215
  53.9 13.9 %collective-permute-start.21 = (f32[256,256]{1,0:T(8,128)S(1)}, f32[256,256]{1,0:T(8,128)S(1)}, u32[]{:S(2)}, u32[]{:S(2)}) collective-permute-start(f32[256,256]{1,0:T(8,128)S(1)} %get-tuple-element.27), channel_id=1, source_target_pairs={{0,8},{1,9},{2,10},{3,11},{4,12},{5,13},{6,14},{7,15},{8,0},{9,1},... | collective-permute-start | bytes 786440 | tf_op jit(solution)/shard_map/ppermute | solution.py:215
  61.1 20.5 %collective-permute-start.1 = (f32[256,256]{1,0:T(8,128)S(1)}, f32[256,256]{1,0:T(8,128)S(1)}, u32[]{:S(2)}, u32[]{:S(2)}) collective-permute-start(f32[256,256]{1,0:T(8,128)S(1)} %shard_map.51.old_ref), channel_id=1, source_target_pairs={{0,8},{1,9},{4,12},{5,13},{10,2},{11,3},{14,6},{15,7},{16,24},{17,... | collective-permute-start | bytes 786440 | tf_op jit(solution)/shard_map/ppermute | solution.py:215
  62.4 22.6 %collective-permute-start.5 = (f32[256,256]{1,0:T(8,128)S(1)}, f32[256,256]{1,0:T(8,128)S(1)}, u32[]{:S(2)}, u32[]{:S(2)}) collective-permute-start(f32[256,256]{1,0:T(8,128)S(1)} %get-tuple-element.18), channel_id=1, source_target_pairs={{0,0},{1,1},{2,8},{3,9},{8,2},{9,3},{10,10},{11,11},{20,20},{21,21... | collective-permute-start | bytes 786440 | tf_op jit(solution)/shard_map/ppermute | solution.py:215
  63.1 22.0 %collective-permute-start.9 = (f32[256,256]{1,0:T(8,128)S(1)}, f32[256,256]{1,0:T(8,128)S(1)}, u32[]{:S(2)}, u32[]{:S(2)}) collective-permute-start(f32[256,256]{1,0:T(8,128)S(1)} %collective-permute-done.8), channel_id=1, source_target_pairs={{0,0},{1,1},{2,8},{3,9},{4,16},{5,17},{6,24},{7,25},{8,2},{9,3},{1... | collective-permute-start | bytes 786440 | tf_op jit(solution)/shard_map/ppermute | solution.py:215
  66.5 18.5 %collective-permute-start.7 = (f32[256,256]{1,0:T(8,128)S(1)}, f32[256,256]{1,0:T(8,128)S(1)}, u32[]{:S(2)}, u32[]{:S(2)}) collective-permute-start(f32[256,256]{1,0:T(8,128)S(1)} %collective-permute-done.6), channel_id=1, source_target_pairs={{0,4},{1,5},{2,12},{3,13},{8,6},{9,7},{10,14},{11,15},{20,16},{21,... | collective-permute-start | bytes 786440 | tf_op jit(solution)/shard_map/ppermute | solution.py:215
  67.9 9.7 %collective-permute-start.22 = (f32[128,256]{1,0:T(8,128)S(1)}, f32[128,256]{1,0:T(8,128)S(1)}, u32[]{:S(2)}, u32[]{:S(2)}) collective-permute-start(f32[128,256]{1,0:T(8,128)S(1)} %get-tuple-element.29), channel_id=1, source_target_pairs={{0,16},{1,17},{2,18},{3,19},{4,20},{5,21},{6,22},{7,23},{8,24},{9,... | collective-permute-start | bytes 393224 | tf_op jit(solution)/shard_map/ppermute | solution.py:215
  77.6 9.3 %collective-permute-start.23 = (f32[64,256]{1,0:T(8,128)S(1)}, f32[64,256]{1,0:T(8,128)S(1)}, u32[]{:S(2)}, u32[]{:S(2)}) collective-permute-start(f32[64,256]{1,0:T(8,128)S(1)} %get-tuple-element.30), channel_id=1, source_target_pairs={{0,0},{1,1},{2,8},{3,9},{4,16},{5,17},{6,24},{7,25},{8,4},{9,5},{1... | collective-permute-start | bytes 196616 | tf_op jit(solution)/shard_map/ppermute | solution.py:215
  81.6 7.4 %collective-permute-start.24 = (f32[64,256]{1,0:T(8,128)S(1)}, f32[64,256]{1,0:T(8,128)S(1)}, u32[]{:S(2)}, u32[]{:S(2)}) collective-permute-start(f32[64,256]{1,0:T(8,128)S(1)} %get-tuple-element.31), channel_id=1, source_target_pairs={{0,1},{1,0},{2,9},{3,8},{4,17},{5,16},{6,25},{7,24},{8,5},{9,4},{1... | collective-permute-start | bytes 196616 | tf_op jit(solution)/shard_map/ppermute | solution.py:215
